TPU v7x, 512 devices: a whole 4x8x8 slice. The times are simulated.
512 devices in a mesh: tm: 16 (over y, z_lo), feed: 32 (over z_hi, x, core).
Axes of the slice: x: 4, y: 8, z: 8 (z_hi: 4, z_lo: 2; z = z_hi * 2 + z_lo), core: 2. Of those that a mesh axis runs over, the one named last changes fastest.
Arguments:
- voltages: int32 [2048, 131072], P('feed', 'tm'), may hold values from -128 to 127
- feed_at_grid_slot: int32 [2048], replicated, may hold values from 0 to 2047, each once
- ew_grid: int32 [4], replicated, may hold values from 0 to 511
- ns_grid: int32 [256], replicated, may hold values from 0 to 511
- delays: int32 [1024, 512], replicated, may hold values from 0 to 63, as said below
Outputs:
- dedispersed: float32 [512, 1024, 64], P('tm', 'feed')
Inputs may be any that keep to these rules, and one draw needn't show every extreme that they name: `feed_at_grid_slot`: each feed stands at exactly one grid position. delays are taken modulo 64.
All inputs are finite; a program needn't handle non-finite values.
Results may differ from a plain program's by a relative error of at most 0.017.
Values may be sent and summed in bfloat16 or wider, within the bound.
No kernel may reach another device: no remote copies, remote signals or barrier semaphores. Data moves between devices by JAX's collectives and lax.ppermute only.
A program may use at most 64 MiB of HBM per device.

v0:
```python
from functools import partial
import math

import jax
import jax.numpy as jnp
from jax import lax
from jax.sharding import PartitionSpec as P

NFFT = 2048
CHANS = 1024
TAPS = 4
ROWS = 256


TWO_PI = 2.0 * math.pi
phase_modulus = 1048576


def from_behind(block, axis, distance):
    devices = range(lax.axis_size(axis))
    route = [(i - distance, i) for i in devices if i - distance in devices]
    return lax.ppermute(block, axis, route)


def pfb_window(tap_count, series_length):
    points = jnp.arange(tap_count * series_length, dtype=jnp.float32) + 0.5
    start_offset = points / series_length - tap_count / 2.0
    taper = 0.5 - 0.5 * jnp.cos(TWO_PI * points / (tap_count * series_length))
    values = (jnp.sinc(start_offset) * taper).reshape(tap_count, series_length)
    return values / jnp.sqrt(jnp.sum(values * values, axis=0, keepdims=True))


def dft_table(series_length, columns):
    product = (
        jnp.arange(series_length, dtype=jnp.int32)[:, None]
        * jnp.arange(columns, dtype=jnp.int32)[None, :]
        % series_length
    )
    angles = product.astype(jnp.float32) * (TWO_PI / series_length)
    factor = 1.0 / math.sqrt(series_length)
    return jnp.concatenate([jnp.cos(angles) * factor, -jnp.sin(angles) * factor], axis=1).astype(
        jnp.bfloat16
    )


def spectral_table(series_length):
    product = (
        jnp.arange(series_length, dtype=jnp.int32)[:, None]
        * jnp.arange(series_length, dtype=jnp.int32)[None, :]
        % series_length
    )
    angles = product.astype(jnp.float32) * (TWO_PI / series_length)
    factor = 1.0 / math.sqrt(series_length)
    nonzero = (jnp.arange(series_length) > 0)[:, None]
    cosine = jnp.where(nonzero, jnp.cos(angles) * factor, 0.0)
    sine_part = jnp.where(nonzero, -jnp.sin(angles) * factor, 0.0)
    return jnp.stack([cosine, sine_part]).astype(jnp.bfloat16)


def steer_table(coords, grid_ids, chan_ids, factor):
    phases = (
        coords[None, None, :] * grid_ids[None, :, None] * chan_ids[:, None, None] % phase_modulus
    )
    angles = phases.astype(jnp.float32) * (TWO_PI / phase_modulus)
    return (
        (jnp.cos(angles) * factor).astype(jnp.bfloat16),
        (jnp.sin(angles) * factor).astype(jnp.bfloat16),
    )


def form_beams(block_in, feed_at_grid_slot, ew_tables, ns_tables):
    ew_real, ew_imag = ew_tables
    ns_real, ns_imag = ns_tables
    item_count = block_in.shape[1]
    chan_count = block_in.shape[3]
    gridded = jnp.take(block_in, feed_at_grid_slot, axis=0).reshape(
        ROWS, 4, 2, item_count, 2, chan_count
    )
    grid_real = gridded[:, :, :, :, 0, :]
    grid_imag = gridded[:, :, :, :, 1, :]
    east_mix = partial(jnp.einsum, "cey,rypsc->erpsc", preferred_element_type=jnp.float32)
    east_real = (east_mix(ew_real, grid_real) - east_mix(ew_imag, grid_imag)).astype(jnp.bfloat16)
    east_imag = (east_mix(ew_real, grid_imag) + east_mix(ew_imag, grid_real)).astype(jnp.bfloat16)
    north_mix = partial(jnp.einsum, "cbr,erpsc->ebpsc", preferred_element_type=jnp.float32)
    beam_real = north_mix(ns_real, east_real) - north_mix(ns_imag, east_imag)
    beam_imag = north_mix(ns_real, east_imag) + north_mix(ns_imag, east_real)
    beam_power = jnp.sum(beam_real * beam_real + beam_imag * beam_imag, axis=2)
    return beam_power.reshape(-1, item_count, chan_count).astype(jnp.bfloat16)


def local(voltages, feed_at_grid_slot, ew_grid, ns_grid, delays):
    feed_dev = voltages.shape[0]
    spec_dev = voltages.shape[1] // NFFT
    time_extent = lax.axis_size("tm")
    feed_size = lax.axis_size("feed")
    spec_total = spec_dev * time_extent
    frames = (
        (voltages.astype(jnp.float32) / 64.0).astype(jnp.bfloat16).reshape(feed_dev, spec_dev, NFFT)
    )
    history = from_behind(frames[:, spec_dev - TAPS + 1 :, :], "tm", 1)
    padded = jnp.concatenate([history, frames], axis=1)
    window = pfb_window(TAPS, NFFT)
    filtered = jnp.zeros((feed_dev, spec_dev, NFFT), jnp.float32)
    for tap_index in range(TAPS):
        filtered = filtered + window[tap_index] * padded[
            :, tap_index : tap_index + spec_dev, :
        ].astype(jnp.float32)
    spectra = jnp.dot(
        filtered.astype(jnp.bfloat16).reshape(feed_dev * spec_dev, NFFT),
        dft_table(NFFT, CHANS),
        preferred_element_type=jnp.float32,
    )
    spectra = spectra.astype(jnp.bfloat16).reshape(feed_dev, spec_dev, 2, CHANS)
    chan_dev = CHANS // feed_size
    chan_ids = lax.axis_index("feed") * chan_dev + jnp.arange(chan_dev, dtype=jnp.int32) + CHANS
    ew_tables = steer_table(jnp.arange(4, dtype=jnp.int32), ew_grid, chan_ids, 0.5)
    ns_tables = steer_table(
        jnp.arange(ROWS, dtype=jnp.int32), ns_grid, chan_ids, 1.0 / math.sqrt(ROWS)
    )
    intensity = form_beams(
        lax.all_to_all(spectra, "feed", split_axis=3, concat_axis=0, tiled=True),
        feed_at_grid_slot,
        ew_tables,
        ns_tables,
    )
    time_table = spectral_table(spec_total)
    first_freq = lax.axis_index("tm") * spec_dev
    by_beam = lax.all_to_all(intensity, "feed", split_axis=0, concat_axis=2, tiled=True)
    my_table = lax.dynamic_slice_in_dim(time_table, first_freq, spec_dev, 1)
    zero_init = jnp.zeros((by_beam.shape[0], 2, spec_dev, CHANS), jnp.float32)
    spectrum = (
        zero_init
        + jnp.einsum(
            "rkt,btc->brkc",
            my_table,
            lax.all_gather(by_beam, "tm", axis=1, tiled=True),
            preferred_element_type=jnp.float32,
        )
    ).astype(jnp.bfloat16)
    freq_ids = first_freq + jnp.arange(spec_dev, dtype=jnp.int32)
    phases = freq_ids[:, None, None] * delays[None, :, :] % spec_total
    angles = phases.astype(jnp.float32) * (TWO_PI / spec_total)
    phase_real = jnp.cos(angles).astype(jnp.bfloat16)
    phase_imag = jnp.sin(angles).astype(jnp.bfloat16)
    shift_mixture = partial(jnp.einsum, "vuw,uwt->vut", preferred_element_type=jnp.float32)
    spec_real = spectrum[:, 0]
    spec_imag = spectrum[:, 1]
    moved_real = shift_mixture(spec_real, phase_real) - shift_mixture(spec_imag, phase_imag)
    moved_imag = shift_mixture(spec_real, phase_imag) + shift_mixture(spec_imag, phase_real)
    folded = (jnp.stack([moved_real, moved_imag], axis=1) * (1.0 / math.sqrt(CHANS))).astype(
        jnp.bfloat16
    )
    combined = lax.all_to_all(folded, "tm", split_axis=3, concat_axis=2, tiled=True)
    return jnp.einsum("brkd,rkt->dbt", combined, time_table, preferred_element_type=jnp.float32)


def solution(mesh):
    in_specs = (P("feed", "tm"), P(), P(), P(), P())
    out_specs = P("tm", "feed", None)
    return jax.shard_map(local, mesh=mesh, in_specs=in_specs, out_specs=out_specs, check_vma=False)
```

profile of v0, /device:TPU:1, one launch (start us, length us, event | category | flops | bytes accessed | tf_op | source)
XLA Modules:
  0.0 552.6 jit_solution(15236078010162098595)
XLA Ops:
  6.5 1.8 multiply_convert_fusion.4
  10.3 4.9 collective-permute-start
  16.0 35.2 %multiply_convert_fusion.2 = (bf16[2048,1024]{1,0:T(8,128)(2,1)}, bf16[2048,1024]{1,0:T(8,128)(2,1)}) fusion(), kind=kLoop, calls=%fused_computation.30 | loop fusion | flops 39845888 | bytes 8388608 | tf_op jit(solution)/shard_map/convert.1
  51.9 3.4 add_convert_fusion
  55.6 5.8 %fusion.32 = bf16[256,2048]{1,0:T(8,128)(2,1)S(1)} fusion(bf16[256,2048]{1,0:T(8,128)(2,1)S(1)} %reshape.210, bf16[2048,1024]{1,0:T(8,128)(2,1)} %get-tuple-element.13, bf16[2048,1024]{1,0:T(8,128)(2,1)} %get-tuple-element.14), kind=kOutput, calls=%fused_computation.48 | convolution fusion | flops 2164785152 | bytes 10485760 | tf_op jit(solution)/shard_map/dot_general | solution.py:108
  62.2 2.3 copy.103
  64.6 2.3 reshape.229
  66.8 13.0 %all-to-all-start = ((bf16[32,2,8192]{2,1,0:T(2,128)(2,1)}), bf16[32,2,8192]{2,1,0:T(2,128)(2,1)S(1)}, u32[]{:S(2)}, u32[]{:S(2)}) async-start(bf16[32,2,8192]{2,1,0:T(2,128)(2,1)} %reshape.229), calls=%async_computation | async-start | bytes 2097152 | tf_op jit(solution)/shard_map/all_to_all | solution.py:121
  81.1 22.7 %all-to-all-done = bf16[32,2,8192]{2,1,0:T(2,128)(2,1)S(1)} async-done(((bf16[32,2,8192]{2,1,0:T(2,128)(2,1)}), bf16[32,2,8192]{2,1,0:T(2,128)(2,1)S(1)}, u32[]{:S(2)}, u32[]{:S(2)}) %all-to-all-start) | async-done | bytes 1048608 | tf_op jit(solution)/shard_map/all_to_all | solution.py:121
  103.8 2.4 reshape.230
  106.1 1.9 copy.104
  108.0 4.8 copy.132
  112.7 18.8 %gather_fusion = bf16[2048,4,2,32]{3,1,2,0:T(4,128)(2,1)} fusion(bf16[2048,4,2,32]{3,1,2,0:T(4,128)(2,1)} %bitcast.106, s32[2048]{0:T(1024)S(1)} %fusion.109), kind=kCustom, calls=%fused_computation | custom fusion | bytes 2105344 | tf_op jit(solution)/shard_map/jit(_take)/gather | solution.py:76
  131.6 7.0 %copy.108 = bf16[256,4,2,4,2,32]{0,1,3,2,5,4:T(4,128)(2,1)S(1)} copy(bf16[256,4,2,4,2,32]{5,3,4,2,1,0:T(4,128)(2,1)} %bitcast.107) | data formatting | bytes 2097152 | tf_op jit(solution)/shard_map/jit(_take)/gather | solution.py:76
  140.7 0.9 fusion.58
  142.6 31.8 %fusion.22 = f32[32,4,2,4,256]{4,3,2,1,0:T(4,128)S(1)} fusion(s32[32]{0:T(128)S(1)} %add_add_fusion, s32[256,256]{1,0:T(8,128)S(1)} %iota_multiply_fusion, bf16[4,256,2,4,32]{1,0,3,2,4:T(4,128)(2,1)S(1)} %fusion.58), kind=kOutput, calls=%fused_computation.41 | convolution fusion | flops 167772160 | bytes 1835136 | tf_op jit(solution)/shard_map/cbr,erpsc->ebpsc/dot_general | solution.py:85
  174.4 32.0 %fusion.20 = f32[32,4,2,4,256]{4,3,2,1,0:T(4,128)S(1)} fusion(s32[32]{0:T(128)S(1)} %add_add_fusion, s32[256,256]{1,0:T(8,128)S(1)} %iota_multiply_fusion, bf16[4,256,2,4,32]{1,0,3,2,4:T(4,128)(2,1)S(1)} %fusion.59), kind=kOutput, calls=%fused_computation.40 | convolution fusion | flops 167772160 | bytes 1835136 | tf_op jit(solution)/shard_map/cbr,erpsc->ebpsc/dot_general | solution.py:86
  206.4 31.5 %fusion.38 = f32[32,4,2,4,256]{4,3,2,1,0:T(4,128)S(1)} fusion(f32[32,4,2,4,256]{4,3,2,1,0:T(4,128)S(1)} %fusion.22, s32[32]{0:T(128)S(1)} %add_add_fusion, s32[256,256]{1,0:T(8,128)S(1)} %iota_multiply_fusion, bf16[4,256,2,4,32]{1,0,3,2,4:T(4,128)(2,1)S(1)} %fusion.59), kind=kOutput, calls=%fused_computation.58 | convolution fusion | flops 168296448 | bytes 2883712 | tf_op jit(solution)/shard_map/cbr,erpsc->ebpsc/dot_general | solution.py:85
  237.9 31.9 %fusion.55 = bf16[32,4,4,256]{3,2,1,0:T(4,128)(2,1)S(1)} fusion(f32[32,4,2,4,256]{4,3,2,1,0:T(4,128)S(1)} %fusion.38, f32[32,4,2,4,256]{4,3,2,1,0:T(4,128)S(1)} %fusion.20, s32[32]{0:T(128)S(1)} %add_add_fusion, s32[256,256]{1,0:T(8,128)S(1)} %iota_multiply_fusion, bf16[4,256,2,4,32]{1,0,3,2,4:T(4,128)(2,1)S(1)} %fusion.58), kind=kOutput, calls=%fused_computation.65 | convolution fusion | flops 168689664 | bytes 3145856 | tf_op jit(solution)/shard_map/cbr,erpsc->ebpsc/dot_general | solution.py:86
  270.5 1.0 reshape.231
  271.5 23.5 %all_to_all.54 = bf16[32,2,2048]{2,1,0:T(2,128)(2,1)S(1)} all-to-all(bf16[32,2,2048]{2,1,0:T(2,128)(2,1)S(1)} %reshape.231), channel_id=1, replica_groups=mesh['tm'=16,'feed'=32] {'feed'}, dimensions={0} | all-to-all | bytes 524288 | tf_op jit(solution)/shard_map/all_to_all | solution.py:128
  296.3 1.8 all_to_all.46
  298.3 94.9 %all-gather.2.cloned.1.call-done = bf16[32,64,1024]{2,0,1:T(8,128)(2,1)} async-done(((bf16[32,4,1024]{2,0,1:T(8,128)(2,1)}), bf16[32,64,1024]{2,0,1:T(8,128)(2,1)}) %all-gather.2.cloned.1.call-update) | async-done | bytes 4194320 | tf_op jit(solution)/shard_map/all_gather | solution.py:136
  393.3 4.6 fusion.60
  398.1 32.4 %fusion.28 = f32[4,512,32]{1,2,0:T(8,128)S(1)} fusion(s32[1024,512]{1,0:T(8,128)} %param.9, s32[4]{0:T(128)S(1)} %iota_add_fusion, bf16[32,4,1024]{2,1,0:T(4,128)(2,1)S(1)} %get-tuple-element.5), kind=kOutput, calls=%fused_computation.44 | convolution fusion | flops 165675008 | bytes 2621456 | tf_op jit(solution)/shard_map/vuw,uwt->vut/dot_general | solution.py:148
  430.5 30.5 %fusion.29 = f32[4,512,32]{1,2,0:T(8,128)S(1)} fusion(s32[1024,512]{1,0:T(8,128)S(1)} %copy-done.3, s32[4]{0:T(128)S(1)} %iota_add_fusion, bf16[32,4,1024]{2,1,0:T(4,128)(2,1)S(1)} %get-tuple-element.6), kind=kOutput, calls=%fused_computation.45 | convolution fusion | flops 165675008 | bytes 2621456 | tf_op jit(solution)/shard_map/vuw,uwt->vut/dot_general | solution.py:149
  461.1 31.2 %fusion.66 = f32[32,1,4,512]{3,0,2,1:T(8,128)S(1)} fusion(f32[4,512,32]{1,2,0:T(8,128)S(1)} %fusion.28, s32[1024,512]{1,0:T(8,128)S(1)} %copy-done.3, s32[4]{0:T(128)S(1)} %iota_add_fusion, bf16[32,4,1024]{2,1,0:T(4,128)(2,1)S(1)} %get-tuple-element.6), kind=kOutput, calls=%fused_computation.73 | convolution fusion | flops 165740544 | bytes 2883600 | tf_op jit(solution)/shard_map/vuw,uwt->vut/dot_general | solution.py:148
  492.2 31.1 %fusion.64 = f32[32,1,4,512]{3,0,2,1:T(8,128)S(1)} fusion(f32[4,512,32]{1,2,0:T(8,128)S(1)} %fusion.29, s32[1024,512]{1,0:T(8,128)S(1)} %copy-done.3, s32[4]{0:T(128)S(1)} %iota_add_fusion, bf16[32,4,1024]{2,1,0:T(4,128)(2,1)S(1)} %get-tuple-element.5), kind=kOutput, calls=%fused_computation.71 | convolution fusion | flops 165740544 | bytes 2883600 | tf_op jit(solution)/shard_map/vuw,uwt->vut/dot_general | solution.py:149
  524.1 1.0 reshape.233
  525.0 17.2 %all_to_all.55 = bf16[16,2,4096]{2,1,0:T(2,128)(2,1)S(1)} all-to-all(bf16[16,2,4096]{2,1,0:T(2,128)(2,1)S(1)} %reshape.233), channel_id=1, replica_groups=mesh['tm'=16,'feed'=32] {'tm'}, dimensions={0} | all-to-all | bytes 524288 | tf_op jit(solution)/shard_map/all_to_all | solution.py:153
  542.8 0.9 copy.123
  544.2 1.1 copy.125
  (43 shorter events, 12.8 us)
Async XLA Ops:
  10.3 40.8 %collective-permute-start = (bf16[64,3,2048]{2,0,1:T(8,128)(2,1)S(1)}, bf16[64,3,2048]{2,0,1:T(8,128)(2,1)S(1)}, u32[]{:S(2)}, u32[]{:S(2)}) collective-permute-start(bf16[64,3,2048]{2,0,1:T(8,128)(2,1)S(1)} %copy.101), channel_id=1, source_target_pairs={{0,32},{32,64},{64,96},{96,128},{128,160},{160,192},{192,224},{224... | collective-permute-start | bytes 2359304 | tf_op jit(solution)/shard_map/ppermute | solution.py:22
  62.2 17.9 %copy-start = (s32[2048]{0:T(1024)S(1)}, s32[2048]{0:T(1024)}, u32[]{:S(2)}) copy-start(s32[2048]{0:T(1024)} %param.6) | copy-start | bytes 24580
  62.2 18.7 %copy-start.2 = (s32[4]{0:T(128)S(1)}, s32[4]{0:T(128)}, u32[]{:S(2)}) copy-start(s32[4]{0:T(128)} %param.7) | copy-start | bytes 52
  62.2 18.8 %copy-start.1 = (s32[256]{0:T(256)S(1)}, s32[256]{0:T(256)}, u32[]{:S(2)}) copy-start(s32[256]{0:T(256)} %param.8) | copy-start | bytes 3076
  66.8 36.9 %all-to-all-start = ((bf16[32,2,8192]{2,1,0:T(2,128)(2,1)}), bf16[32,2,8192]{2,1,0:T(2,128)(2,1)S(1)}, u32[]{:S(2)}, u32[]{:S(2)}) async-start(bf16[32,2,8192]{2,1,0:T(2,128)(2,1)} %reshape.229), calls=%async_computation | async-start | bytes 2097152 | tf_op jit(solution)/shard_map/all_to_all | solution.py:121
  79.8 313.4 %all-gather.2.cloned.1.call-start = ((), (), s32[]{:S(2)}) async-start(), calls=%async_computation.3 | async-start | bytes 4456448 | tf_op jit(solution)/shard_map/all_gather | solution.py:136
  398.0 32.5 %copy-start.3 = (s32[1024,512]{1,0:T(8,128)S(1)}, s32[1024,512]{1,0:T(8,128)}, u32[]{:S(2)}) copy-start(s32[1024,512]{1,0:T(8,128)} %param.9) | copy-start | bytes 6291460
Sparse Core Ops, SparseCore 0:
  298.2 94.9 all-gather.1
where the time goes:
time: 562 us; the launch traced here: 553 us
  matrix products  267 us (48%)
  waiting for transfers between devices  118 us (21%)
  local copies, waits for them, and re-layouts  53.1 us (9%)
  other arithmetic  42 us (7%)
  blocking collectives  40.8 us (7%)
  starting transfers between devices  18.1 us (3%)
  between operations  14.2 us (3%)
    all_gather x1, waiting for transfers between devices, local(): lax.all_gather(by_beam, 'tm', axis=1, tiled=True)  94.9 us
    dot_general x2, matrix products, form_beams(): beam_imag = north_mix(ns_real, east_imag) + north_mix(ns_imag, east_real)  63.9 us
    dot_general x2, matrix products, form_beams(): beam_real = north_mix(ns_real, east_real) - north_mix(ns_imag, east_imag)  63.3 us
    another operation x2, other arithmetic  35.4 us
    dot_general x1, matrix products, local(): shift_mixture(spec_real, phase_real) - shift_mixture(spec_imag, phase_imag)  32.4 us
    dot_general x1, matrix products, local(): shift_mixture(spec_imag, phase_imag)  31.2 us
    dot_general x1, matrix products, local(): shift_mixture(spec_real, phase_imag) + shift_mixture(spec_imag, phase_real)  31.1 us
    dot_general x1, matrix products, local(): shift_mixture(spec_imag, phase_real)  30.5 us
  transfers between devices with their start and end apart: 3, of which 2 were waited for; matrix products, arithmetic and copies ran while one was open for 7% of the time, Pallas kernels for 0%

commit v1 on v0

v1 whole, which is shorter than its diff:
```python
import math
from functools import partial

import jax
import jax.numpy as jnp
from jax import lax
from jax.experimental import pallas as pl
from jax.experimental.pallas import tpu as pltpu
from jax.sharding import PartitionSpec as P

NFFT = 2048
CHANS = 1024
TAPS = 4
ROWS = 256
SPECTRA = 64
HALF = NFFT // 2
TWO_PI = 2.0 * math.pi
PHASE_MODULUS = 1048576
F32 = jnp.float32
BF16 = jnp.bfloat16
NT = (((1,), (1,)), ((), ()))


def iota(shape, axis):
    return lax.broadcasted_iota(jnp.int32, shape, axis)


def pfb_window():
    points = jnp.arange(TAPS * NFFT, dtype=F32) + 0.5
    start_offset = points / NFFT - TAPS / 2.0
    taper = 0.5 - 0.5 * jnp.cos(TWO_PI * points / (TAPS * NFFT))
    values = (jnp.sinc(start_offset) * taper).reshape(TAPS, NFFT)
    return values / jnp.sqrt(jnp.sum(values * values, axis=0, keepdims=True))


def twiddle_tables():
    coarse = iota((32, HALF), 0) * iota((32, HALF), 1) % 64
    coarse = coarse.astype(F32) * (TWO_PI / 64)
    shape = (2, 32, HALF)
    row = iota(shape, 1)
    chan = (row // 2) * 2 + iota(shape, 0)
    fine = (chan * iota(shape, 2) + (row % 2) * 512) % NFFT
    fine = fine.astype(F32) * (TWO_PI / NFFT)
    factor = 1.0 / math.sqrt(NFFT)
    seeds = (jnp.cos(coarse), jnp.sin(coarse), jnp.cos(fine) * factor, jnp.sin(fine) * factor)
    cos_a, sin_a, cos_b, sin_b = lax.optimization_barrier(seeds)
    table = cos_a[None, :, None, :] * cos_b[:, None] - sin_a[None, :, None, :] * sin_b[:, None]
    return table.astype(BF16).reshape(2, 1024, HALF)


def steer_seed(steps, grid_ids, chan_ids, factor):
    phases = steps[None, :, None] * grid_ids[None, None, :] * chan_ids[:, None, None] % PHASE_MODULUS
    angles = phases.astype(F32) * (TWO_PI / PHASE_MODULUS)
    return jnp.cos(angles) * factor, jnp.sin(angles) * factor


def north_tables(ns_grid, chan_ids):
    steps = jnp.arange(16, dtype=jnp.int32)
    seeds = steer_seed(steps * 16, ns_grid, chan_ids, 1.0) + steer_seed(steps, ns_grid, chan_ids, 1.0 / math.sqrt(ROWS))
    cos_a, sin_a, cos_b, sin_b = lax.optimization_barrier(seeds)
    cos_a, sin_a = cos_a[:, :, None, :], sin_a[:, :, None, :]
    cos_b, sin_b = cos_b[:, None], sin_b[:, None]
    real = (cos_a * cos_b - sin_a * sin_b).astype(BF16).reshape(2, ROWS, 256)
    imag = (sin_a * cos_b + cos_a * sin_b).astype(BF16).reshape(2, ROWS, 256)
    return jnp.concatenate([real, imag], axis=2)


def time_rows():
    block = jnp.arange(16, dtype=jnp.int32)
    ks = jnp.stack([block + 1, jnp.where(block == 15, 32, 31 - block)])
    product = ks[:, :, None] * jnp.arange(SPECTRA, dtype=jnp.int32) % SPECTRA
    angles = product.astype(F32) * (TWO_PI / SPECTRA)
    factor = 1.0 / math.sqrt(SPECTRA)
    table = jnp.stack([jnp.cos(angles) * factor, -jnp.sin(angles) * factor], axis=1)
    weight = jnp.where(ks == 32, 1.0, 2.0)[:, None, :, None]
    table = table.astype(BF16)
    return table.reshape(64, SPECTRA), (table * weight.astype(BF16)).reshape(4, 16, SPECTRA)


def channelize_kernel(v_ref, h_ref, w_ref, t_ref, o_ref, x_ref):
    @pl.when(pl.program_id(0) == 0)
    def _():
        for s in range(4):
            total = None
            for tap in range(TAPS):
                at = s + tap - 3
                if at < 0:
                    frame = h_ref[:, (at + 3) * NFFT : (at + 4) * NFFT].astype(F32)
                else:
                    frame = v_ref[:, at * NFFT : (at + 1) * NFFT].astype(F32)
                term = w_ref[tap : tap + 1, :] * frame
                total = term if total is None else total + term
            low, high = total[:, :HALF], total[:, HALF:]
            x_ref[0, s * 64 : (s + 1) * 64, :] = (low + high).astype(BF16)
            x_ref[1, s * 64 : (s + 1) * 64, :] = (low - high).astype(BF16)

    parity = pl.program_id(0) // 4
    acc = lax.dot_general(t_ref[...], x_ref[parity], NT, preferred_element_type=F32)
    first = acc[:, :128].reshape(32, 8, 128)
    second = acc[:, 128:].reshape(32, 8, 128)
    upper = iota((32, 8, 128), 1) < 4
    even = jnp.where(upper, first, pltpu.roll(second, 4, 1))
    odd = jnp.where(upper, pltpu.roll(first, 4, 1), second)
    o_ref[:, 0] = even.astype(BF16)
    o_ref[:, 1] = odd.astype(BF16)


def channelize(voltages, halo, window, table):
    out = pl.pallas_call(
        channelize_kernel,
        grid=(8,),
        in_specs=[
            pl.BlockSpec((64, 4 * NFFT), lambda i: (0, 0)),
            pl.BlockSpec((64, 3 * NFFT), lambda i: (0, 0)),
            pl.BlockSpec((TAPS, NFFT), lambda i: (0, 0)),
            pl.BlockSpec((256, HALF), lambda i: (i, 0)),
        ],
        out_specs=pl.BlockSpec((32, 2, 8, 128), lambda i: (i, 0, 0, 0)),
        out_shape=jax.ShapeDtypeStruct((256, 2, 8, 128), BF16),
        scratch_shapes=[pltpu.VMEM((2, 256, HALF), BF16)],
        name="channelize",
    )(voltages, halo, window, table.reshape(2048, HALF))
    return out.reshape(512, 8, 128)


def beam_kernel(r_ref, slot_ref, ns_ref, ew_ref, time_ref, o_ref, z_ref, x_ref, y_ref):
    left = iota((128, 128), 1) < 64

    def assemble(g, _):
        first = r_ref[:, 2 * g].astype(F32).reshape(128, 128)
        second = r_ref[:, 2 * g + 1].astype(F32).reshape(128, 128)
        lanes = pl.ds(pl.multiple_of(g * 128, 128), 128)
        z_ref[0:128, lanes] = jnp.where(left, first, pltpu.roll(second, 64, 1)).astype(BF16)
        z_ref[128:256, lanes] = jnp.where(left, pltpu.roll(first, 64, 1), second).astype(BF16)
        return 0

    lax.fori_loop(0, 16, assemble, 0)
    row = iota((256, 256), 0)
    time = row % 64
    source = (time % 2) * 128 + (time // 4) * 8 + ((time // 2) % 2) * 4 + row // 64
    order = jnp.where(source == iota((256, 256), 1), 1.0, 0.0).astype(BF16)
    x_ref[...] = jnp.dot(order, z_ref[...], preferred_element_type=F32).astype(BF16)

    def north(cp, _):
        slots = slot_ref[pl.ds(cp, 1), :]
        select = jnp.where(iota((2048, 256), 0) == slots, 1.0, 0.0).astype(BF16)
        grid = jnp.dot(x_ref[...], select, preferred_element_type=F32).astype(BF16)
        for c in range(2):
            both = jnp.dot(grid[c * 128 : (c + 1) * 128], ns_ref[c], preferred_element_type=F32)
            y_ref[c, cp, 0] = both[:64, :256] - both[64:, 256:]
            y_ref[c, cp, 1] = both[64:, :256] + both[:64, 256:]
        return 0

    lax.fori_loop(0, 8, north, 0)
    for c in range(2):

        def east(e, _):
            power = None
            for pol in range(2):
                real, imag = None, None
                for cyl in range(4):
                    w_re = ew_ref[0, c * 16 + e * 4 + cyl]
                    w_im = ew_ref[1, c * 16 + e * 4 + cyl]
                    y_re = y_ref[c, 2 * cyl + pol, 0]
                    y_im = y_ref[c, 2 * cyl + pol, 1]
                    re = w_re * y_re - w_im * y_im
                    im = w_re * y_im + w_im * y_re
                    real = re if real is None else real + re
                    imag = im if imag is None else imag + im
                part = real * real + imag * imag
                power = part if power is None else power + part
            freq = jnp.dot(time_ref[...], power.astype(BF16), preferred_element_type=F32)
            o_ref[c, e] = freq.astype(BF16)
            return 0

        lax.fori_loop(0, 4, east, 0)


def form_beams(received, slots, ns_table, ew_table, time_table):
    vmem = pl.BlockSpec(memory_space=pltpu.VMEM)
    return pl.pallas_call(
        beam_kernel,
        in_specs=[vmem, vmem, vmem, pl.BlockSpec(memory_space=pltpu.SMEM), vmem],
        out_specs=vmem,
        out_shape=jax.ShapeDtypeStruct((2, 4, 64, 256), BF16),
        scratch_shapes=[
            pltpu.VMEM((256, 2048), BF16),
            pltpu.VMEM((256, 2048), BF16),
            pltpu.VMEM((2, 8, 2, 64, 256), F32),
        ],
        compiler_params=pltpu.CompilerParams(vmem_limit_bytes=48 << 20),
        name="beams",
    )(received, slots, ns_table, ew_table, time_table)


def search_kernel(num_ref, f_ref, d_ref, lut_ref, o_ref, ft_ref):
    @pl.when(pl.program_id(0) == 0)
    def _():
        ft_ref[...] = f_ref[...].astype(F32).T.astype(BF16)

    first_k = num_ref[0]
    last = num_ref[1]
    plain = last.astype(F32)
    scale = 1.0 - plain
    sums = [None, None]
    for parity in range(2):
        delays = d_ref[pl.ds(parity, 512, stride=2), :]
        turn = (first_k * delays) % SPECTRA
        cos = jnp.take_along_axis(jnp.broadcast_to(lut_ref[0:1, :], (512, 128)), turn, axis=1)
        sin = jnp.take_along_axis(jnp.broadcast_to(lut_ref[1:2, :], (512, 128)), turn, axis=1)
        sign = (1 - 2 * (delays % 2)).astype(F32)
        tables = (
            jnp.concatenate([cos.astype(BF16), sin.astype(BF16)], axis=1),
            jnp.concatenate(
                [(sign * (plain + scale * cos)).astype(BF16), (-scale * sign * sin).astype(BF16)], axis=1
            ),
        )
        for pair in range(2):
            part = jnp.dot(
                ft_ref[pair * 64 : (pair + 1) * 64, parity * 512 : (parity + 1) * 512],
                tables[pair],
                preferred_element_type=F32,
            )
            sums[pair] = part if sums[pair] is None else sums[pair] + part
    moved = []
    for pair in range(2):
        both = sums[pair]
        moved.append(both[:32, :128] - both[32:, 128:])
        moved.append(both[:32, 128:] + both[32:, :128])
    moved = jnp.concatenate(moved, axis=0) * (1.0 / math.sqrt(CHANS))
    o_ref[...] = moved.T.astype(BF16)


def search(numbers, freq, delays, lut):
    return pl.pallas_call(
        search_kernel,
        grid=(4,),
        in_specs=[
            pl.BlockSpec(memory_space=pltpu.SMEM),
            pl.BlockSpec((CHANS, 128), lambda i: (0, 0)),
            pl.BlockSpec((CHANS, 128), lambda i: (0, i)),
            pl.BlockSpec((8, 128), lambda i: (0, 0)),
        ],
        out_specs=pl.BlockSpec((128, 128), lambda i: (i, 0)),
        out_shape=jax.ShapeDtypeStruct((512, 128), BF16),
        scratch_shapes=[pltpu.VMEM((128, CHANS), BF16)],
        name="search",
    )(numbers, freq, delays, lut)


def local(voltages, feed_at_grid_slot, ew_grid, ns_grid, delays):
    tm = lax.axis_index("tm")
    me = tm * 32 + lax.axis_index("feed")
    everyone = ("tm", "feed")
    tail = voltages[:, NFFT:].astype(BF16)
    halo = lax.ppermute(tail, "tm", [(i, i + 1) for i in range(15)])
    window = pfb_window() * (1.0 / 64.0)
    spectra = channelize(voltages, halo, window, twiddle_tables())
    received = lax.all_to_all(spectra, everyone, split_axis=0, concat_axis=0, tiled=True)

    chan_ids = (me % 256) * 4 + me // 256 + 2 * jnp.arange(2, dtype=jnp.int32) + CHANS
    ew = steer_seed(jnp.arange(4, dtype=jnp.int32), ew_grid, chan_ids, 0.5)
    ew = jnp.stack([x.astype(BF16).astype(F32).transpose(0, 2, 1).reshape(32) for x in ew])
    slots = feed_at_grid_slot.reshape(ROWS, 8).T
    forward, backward = time_rows()
    freq = form_beams(
        received.reshape(16, 32, 8, 128), slots, north_tables(ns_grid, chan_ids), ew, forward
    )
    freq = freq.reshape(2, 4, 4, 16, 8, 32).transpose(3, 1, 4, 0, 2, 5).reshape(512, 2, 128)
    by_freq = lax.all_to_all(freq, everyone, split_axis=0, concat_axis=0, tiled=True)

    angles = jnp.arange(128, dtype=jnp.int32) % SPECTRA
    angles = angles.astype(F32) * (TWO_PI / SPECTRA)
    lut = jnp.stack([jnp.cos(angles), jnp.sin(angles)] + [jnp.zeros_like(angles)] * 6)
    numbers = jnp.stack([tm + 1, jnp.where(tm == 15, 1, 0)]).astype(jnp.int32)
    moved = search(numbers, by_freq.reshape(CHANS, 128), delays, lut)
    combined = lax.all_to_all(moved.reshape(16, 32, 128), "tm", split_axis=0, concat_axis=0, tiled=True)
    combined = combined.reshape(16, 32, 4, 32)
    return jnp.einsum("gdqb,qgt->dbt", combined, backward, preferred_element_type=F32)


def solution(mesh):
    in_specs = (P("feed", "tm"), P(), P(), P(), P())
    out_specs = P("tm", "feed", None)
    return jax.shard_map(local, mesh=mesh, in_specs=in_specs, out_specs=out_specs, check_vma=False)
```

time: 562 us -> 151 us (0.27); the launches traced: 553 us -> 150 us
  matrix products: 267 us -> 1.29 us
  waiting for transfers between devices: 118 us -> 62.3 us
  local copies, waits for them, and re-layouts: 53.1 us -> 5.96 us
  blocking collectives: 40.8 us -> 0 us
  other arithmetic: 42 us -> 11.2 us
  Pallas kernels: 0 us -> 25.4 us
  starting transfers between devices: 18.1 us -> 43.5 us
  between operations: 14.2 us -> 0.24 us
    dot_general x15 -> x1, matrix products: 267 us -> 1.29 us  [local(): jnp.einsum('gdqb,qgt->dbt', combined, backward, preferred_element_type=F32)]
    all_gather x1 -> x0, waiting for transfers between devices: 94.9 us -> none  [local(): lax.all_gather(by_beam, 'tm', axis=1, tiled=True)]
    all_to_all x2 -> x0, blocking collectives: 40.8 us -> none  [the longest x1 23.5 us: local(): lax.all_to_all(intensity, 'feed', split_axis=0, concat_axis=2, tiled=True)]
    all_to_all x1 -> x3, waiting for transfers between devices: 22.7 us -> 56.8 us  [the longest x1 32.3 us: local(): lax.all_to_all(spectra, everyone, split_axis=0, concat_axis=0, tiled=True)]
    another operation x2 -> x5, other arithmetic: 35.4 us -> 2.83 us
    gather x2 -> x0, local copies, waits for them, and re-layouts: 25.9 us -> none  [form_beams(): jnp.take(block_in, feed_at_grid_slot, axis=0)]
    all_to_all x1 -> x3, starting transfers between devices: 13 us -> 38.7 us  [the longest x1 26.8 us: local(): lax.all_to_all(spectra, everyone, split_axis=0, concat_axis=0, tiled=True)]
    pallas_call x0 -> x3, Pallas kernels: none -> 25.4 us  [the longest x1 10.3 us: form_beams(): pl.pallas_call(beam_kernel, in_specs=[vmem, vmem, vmem, pl.BlockSpec(memo...]
  transfers between devices with their start and end apart: 3 -> 4, of which waited for: 2 -> 4; matrix products, arithmetic and copies ran while one was open for 7% -> 7% of each run, Pallas kernels for 0% -> 0%
where the time goes in v1:
time: 151 us; the launch traced here: 150 us
  waiting for transfers between devices  62.3 us (41%)
  starting transfers between devices  43.5 us (29%)
  Pallas kernels  25.4 us (17%)
  other arithmetic  11.2 us (7%)
  local copies, waits for them, and re-layouts  5.96 us (4%)
    all_to_all x1, waiting for transfers between devices, local(): lax.all_to_all(spectra, everyone, split_axis=0, concat_axis=0, tiled=True)  32.3 us
    all_to_all x1, starting transfers between devices, local(): lax.all_to_all(spectra, everyone, split_axis=0, concat_axis=0, tiled=True)  26.8 us
    all_to_all x1, waiting for transfers between devices, local(): lax.all_to_all(freq, everyone, split_axis=0, concat_axis=0, tiled=True)  15.7 us
    pallas_call x1, Pallas kernels, form_beams(): pl.pallas_call(beam_kernel, in_specs=[vmem, vmem, vmem, pl.BlockSpec(memo...  10.3 us
    pallas_call x1, Pallas kernels, channelize(): pl.pallas_call(channelize_kernel, grid=(8,), in_specs=[pl.BlockSpec((64,...  8.92 us
    all_to_all x1, waiting for transfers between devices, local(): lax.all_to_all(moved.reshape(16, 32, 128), 'tm', split_axis=0, concat_axi...  8.79 us
    all_to_all x1, starting transfers between devices, local(): lax.all_to_all(freq, everyone, split_axis=0, concat_axis=0, tiled=True)  8.38 us
    pallas_call x1, Pallas kernels, search(): pl.pallas_call(search_kernel, grid=(4,), in_specs=[pl.BlockSpec(memory_sp...  6.12 us
  transfers between devices with their start and end apart: 4, of which 4 were waited for; matrix products, arithmetic and copies ran while one was open for 7% of the time, Pallas kernels for 0%

profile of v1, /device:TPU:1, one launch (start us, length us, event | category | flops | bytes accessed | tf_op | source)
XLA Modules:
  0.0 150.0 jit_solution(988583284882562331)
XLA Ops:
  0.0 1.5 slice_convert_fusion
  1.5 4.9 %collective-permute-start = (bf16[64,6144]{1,0:T(8,128)(2,1)S(1)}, bf16[64,6144]{1,0:T(8,128)(2,1)S(1)}, u32[]{:S(2)}, u32[]{:S(2)}) collective-permute-start(bf16[64,6144]{1,0:T(8,128)(2,1)S(1)} %slice_convert_fusion), channel_id=1, source_target_pairs={{0,32},{32,64},{64,96},{96,128},{128,160},{160,192},{192,224},{224... | collective-permute-start | bytes 2359304 | tf_op jit(solution)/shard_map/ppermute | solution.py:256
  6.4 0.4 multiply_reduce_fusion
  6.7 0.5 fusion.10
  7.4 1.1 sine_multiply_fusion
  8.5 0.8 reshape.394
  9.4 0.8 iota_multiply_fusion
  10.1 3.5 %subtract_convert_fusion = bf16[2,32,32,1024]{3,2,1,0:T(8,128)(2,1)} fusion(f32[2,32,1024]{2,1,0:T(8,128)S(1)} %get-tuple-element.16, f32[32,1024]{1,0:T(8,128)S(1)} %get-tuple-element.15, f32[2,32,1024]{2,1,0:T(8,128)S(1)} %get-tuple-element.14, f32[32,1024]{1,0:T(8,128)S(1)} %get-tuple-element.13), kind=kLoop, calls=%fused_computation | loop fusion | flops 8388608 | bytes 4980736 | tf_op jit(solution)/shard_map/convert_element_type | solution.py:48
  13.6 1.0 divide_multiply_fusion.w_ref
  14.6 5.6 %collective-permute-done.h_ref = bf16[64,6144]{1,0:T(8,128)(2,1)S(1)} collective-permute-done((bf16[64,6144]{1,0:T(8,128)(2,1)S(1)}, bf16[64,6144]{1,0:T(8,128)(2,1)S(1)}, u32[]{:S(2)}, u32[]{:S(2)}) %collective-permute-start) | collective-permute-done | bytes 786464 | tf_op jit(solution)/shard_map/ppermute | solution.py:256
  20.2 0.9 copy-done.1
  21.1 8.9 %channelize.1 = bf16[256,2,8,128]{3,2,1,0:T(8,128)(2,1)} custom-call(s32[64,8192]{1,0:T(8,128)} %v_ref.1, bf16[64,6144]{1,0:T(8,128)(2,1)} %copy-done.1, f32[4,2048]{1,0:T(4,128)} %divide_multiply_fusion.w_ref, bf16[2048,1024]{1,0:T(8,128)(2,1)} %bitcast.26), custom_call_target="tpu_custom_call" | custom-call | tf_op jit(solution)/shard_map/channelize/pallas_call | solution.py:109
  30.0 26.8 %all-to-all-start = ((bf16[512,8,128]{2,1,0:T(8,128)(2,1)}), bf16[512,8,128]{2,1,0:T(8,128)(2,1)S(1)}, u32[]{:S(2)}, u32[]{:S(2)}) async-start(bf16[512,8,128]{2,1,0:T(8,128)(2,1)} %bitcast.28), calls=%async_computation | async-start | bytes 2097152 | tf_op jit(solution)/shard_map/all_to_all | solution.py:259
  56.8 0.3 sine_multiply_fusion.1
  57.3 0.1 mul.567
  57.5 0.2 cosine_multiply_fusion.2
  57.7 0.2 subtract_convert_fusion.1
  57.9 32.3 %all-to-all-done = bf16[512,8,128]{2,1,0:T(8,128)(2,1)S(1)} async-done(((bf16[512,8,128]{2,1,0:T(8,128)(2,1)}), bf16[512,8,128]{2,1,0:T(8,128)(2,1)S(1)}, u32[]{:S(2)}, u32[]{:S(2)}) %all-to-all-start) | async-done | bytes 1048608 | tf_op jit(solution)/shard_map/all_to_all | solution.py:259
  90.2 10.3 %beams.1 = bf16[2,4,64,256]{3,2,1,0:T(8,128)(2,1)S(1)} custom-call(bf16[16,32,8,128]{3,2,1,0:T(8,128)(2,1)S(1)} %bitcast.23, s32[8,256]{1,0:T(8,128)S(1)} %bitcast.25, bf16[2,256,512]{2,1,0:T(8,128)(2,1)S(1)} %pad_maximum_fusion.ns_ref, f32[2,32]{1,0:T(2,128)S(1)} %maximum_convert_fusion.1.ew_ref, bf16[64,64]{1,0:T(8,128)(2,1)S(1)} %bitcast.24), custom_call_target="tpu_custom_call" | custom-call | tf_op jit(solution)/shard_map/beams/pallas_call | solution.py:181
  100.5 0.4 reshape.395
  100.9 1.4 copy.8
  102.3 1.2 reshape.396
  103.5 8.4 %all-to-all-start.1 = ((bf16[512,2,128]{2,1,0:T(2,128)(2,1)}), bf16[512,2,128]{2,1,0:T(2,128)(2,1)S(1)}, u32[]{:S(2)}, u32[]{:S(2)}) async-start(bf16[512,2,128]{2,1,0:T(2,128)(2,1)} %reshape.396), calls=%async_computation.1 | async-start | bytes 524288 | tf_op jit(solution)/shard_map/all_to_all | solution.py:270
  112.1 0.7 pad_add_fusion.1.num_ref
  112.8 0.7 maximum_maximum_fusion.lut_ref
  113.5 15.7 %all-to-all-done.1 = bf16[512,2,128]{2,1,0:T(2,128)(2,1)S(1)} async-done(((bf16[512,2,128]{2,1,0:T(2,128)(2,1)}), bf16[512,2,128]{2,1,0:T(2,128)(2,1)S(1)}, u32[]{:S(2)}, u32[]{:S(2)}) %all-to-all-start.1) | async-done | bytes 262176 | tf_op jit(solution)/shard_map/all_to_all | solution.py:270
  129.2 0.7 copy-done
  129.9 6.1 %search.1 = bf16[512,128]{1,0:T(8,128)(2,1)} custom-call(s32[2]{0:T(128)} %pad_add_fusion.1.num_ref, bf16[1024,128]{1,0:T(8,128)(2,1)} %bitcast.31, s32[1024,512]{1,0:T(8,128)} %d_ref.1, f32[8,128]{1,0:T(8,128)} %maximum_maximum_fusion.lut_ref), custom_call_target="tpu_custom_call" | custom-call | tf_op jit(solution)/shard_map/search/pallas_call | solution.py:235
  136.0 3.5 %all-to-all-start.2 = ((bf16[16,32,128]{2,1,0:T(8,128)(2,1)}), bf16[16,32,128]{2,1,0:T(8,128)(2,1)S(1)}, u32[]{:S(2)}, u32[]{:S(2)}) async-start(bf16[16,32,128]{2,1,0:T(8,128)(2,1)} %bitcast.32), calls=%async_computation.2 | async-start | bytes 262144 | tf_op jit(solution)/shard_map/all_to_all | solution.py:277
  139.6 8.8 %all-to-all-done.2 = bf16[16,32,128]{2,1,0:T(8,128)(2,1)S(1)} async-done(((bf16[16,32,128]{2,1,0:T(8,128)(2,1)}), bf16[16,32,128]{2,1,0:T(8,128)(2,1)S(1)}, u32[]{:S(2)}, u32[]{:S(2)}) %all-to-all-start.2) | async-done | bytes 131104 | tf_op jit(solution)/shard_map/all_to_all | solution.py:277
  148.4 0.2 reshape.399
  148.7 1.3 convolution_bitcast_fusion
  (28 shorter events, 0.7 us)
Async XLA Ops:
  1.5 18.7 %collective-permute-start = (bf16[64,6144]{1,0:T(8,128)(2,1)S(1)}, bf16[64,6144]{1,0:T(8,128)(2,1)S(1)}, u32[]{:S(2)}, u32[]{:S(2)}) collective-permute-start(bf16[64,6144]{1,0:T(8,128)(2,1)S(1)} %slice_convert_fusion), channel_id=1, source_target_pairs={{0,32},{32,64},{64,96},{96,128},{128,160},{160,192},{192,224},{224... | collective-permute-start | bytes 2359304 | tf_op jit(solution)/shard_map/ppermute | solution.py:256
  20.2 0.9 copy-start.1
  21.1 36.0 %copy-start.2 = (s32[4]{0:T(128)S(1)}, s32[4]{0:T(128)}, u32[]{:S(2)}) copy-start(s32[4]{0:T(128)} %param.7) | copy-start | bytes 52
  30.0 60.2 %all-to-all-start = ((bf16[512,8,128]{2,1,0:T(8,128)(2,1)}), bf16[512,8,128]{2,1,0:T(8,128)(2,1)S(1)}, u32[]{:S(2)}, u32[]{:S(2)}) async-start(bf16[512,8,128]{2,1,0:T(8,128)(2,1)} %bitcast.28), calls=%async_computation | async-start | bytes 2097152 | tf_op jit(solution)/shard_map/all_to_all | solution.py:259
  103.5 25.7 %all-to-all-start.1 = ((bf16[512,2,128]{2,1,0:T(2,128)(2,1)}), bf16[512,2,128]{2,1,0:T(2,128)(2,1)S(1)}, u32[]{:S(2)}, u32[]{:S(2)}) async-start(bf16[512,2,128]{2,1,0:T(2,128)(2,1)} %reshape.396), calls=%async_computation.1 | async-start | bytes 524288 | tf_op jit(solution)/shard_map/all_to_all | solution.py:270
  129.2 0.7 copy-start
  136.0 12.4 %all-to-all-start.2 = ((bf16[16,32,128]{2,1,0:T(8,128)(2,1)}), bf16[16,32,128]{2,1,0:T(8,128)(2,1)S(1)}, u32[]{:S(2)}, u32[]{:S(2)}) async-start(bf16[16,32,128]{2,1,0:T(8,128)(2,1)} %bitcast.32), calls=%async_computation.2 | async-start | bytes 262144 | tf_op jit(solution)/shard_map/all_to_all | solution.py:277

commit v2 on v1

v2 whole, which is shorter than its diff:
```python
import math
from functools import partial

import jax
import jax.numpy as jnp
from jax import lax
from jax.experimental import pallas as pl
from jax.experimental.pallas import tpu as pltpu
from jax.sharding import PartitionSpec as P

NFFT = 2048
CHANS = 1024
TAPS = 4
ROWS = 256
SPECTRA = 64
HALF = NFFT // 2
TWO_PI = 2.0 * math.pi
PHASE_MODULUS = 1048576
F32 = jnp.float32
BF16 = jnp.bfloat16
NT = (((1,), (1,)), ((), ()))


VMEM = pl.BlockSpec(memory_space=pltpu.VMEM)
SMEM = pl.BlockSpec(memory_space=pltpu.SMEM)
LEAN = pltpu.CompilerParams(vmem_limit_bytes=24 << 20)


def iota(shape, axis):
    return lax.broadcasted_iota(jnp.int32, shape, axis)


def pfb_window():
    points = jnp.arange(TAPS * NFFT, dtype=F32) + 0.5
    start_offset = points / NFFT - TAPS / 2.0
    taper = 0.5 - 0.5 * jnp.cos(TWO_PI * points / (TAPS * NFFT))
    values = (jnp.sinc(start_offset) * taper).reshape(TAPS, NFFT)
    return values / jnp.sqrt(jnp.sum(values * values, axis=0, keepdims=True))


def twiddle_tables():
    coarse = iota((32, HALF), 0) * iota((32, HALF), 1) % 64
    coarse = coarse.astype(F32) * (TWO_PI / 64)
    shape = (2, 32, HALF)
    row = iota(shape, 1)
    chan = (row // 2) * 2 + iota(shape, 0)
    fine = (chan * iota(shape, 2) + (row % 2) * 512) % NFFT
    fine = fine.astype(F32) * (TWO_PI / NFFT)
    factor = 1.0 / math.sqrt(NFFT)
    seeds = (jnp.cos(coarse), jnp.sin(coarse), jnp.cos(fine) * factor, jnp.sin(fine) * factor)
    cos_a, sin_a, cos_b, sin_b = lax.optimization_barrier(seeds)
    table = cos_a[None, :, None, :] * cos_b[:, None] - sin_a[None, :, None, :] * sin_b[:, None]
    return table.astype(BF16).reshape(2, 1024, HALF)


def steer_seed(steps, grid_ids, chan_ids, factor):
    phases = steps[None, :, None] * grid_ids[None, None, :] * chan_ids[:, None, None] % PHASE_MODULUS
    angles = phases.astype(F32) * (TWO_PI / PHASE_MODULUS)
    return jnp.cos(angles) * factor, jnp.sin(angles) * factor


def north_tables(ns_grid, chan_ids):
    steps = jnp.arange(16, dtype=jnp.int32)
    seeds = steer_seed(steps * 16, ns_grid, chan_ids, 1.0) + steer_seed(steps, ns_grid, chan_ids, 1.0 / math.sqrt(ROWS))
    cos_a, sin_a, cos_b, sin_b = lax.optimization_barrier(seeds)
    cos_a, sin_a = cos_a[:, :, None, :], sin_a[:, :, None, :]
    cos_b, sin_b = cos_b[:, None], sin_b[:, None]
    real = (cos_a * cos_b - sin_a * sin_b).astype(BF16).reshape(2, ROWS, 256)
    imag = (sin_a * cos_b + cos_a * sin_b).astype(BF16).reshape(2, ROWS, 256)
    return jnp.concatenate([real, imag], axis=2)


def time_rows():
    block = jnp.arange(16, dtype=jnp.int32)
    ks = jnp.stack([block + 1, jnp.where(block == 15, 32, 31 - block)])
    product = ks[:, :, None] * jnp.arange(SPECTRA, dtype=jnp.int32) % SPECTRA
    angles = product.astype(F32) * (TWO_PI / SPECTRA)
    factor = 1.0 / math.sqrt(SPECTRA)
    table = jnp.stack([jnp.cos(angles) * factor, -jnp.sin(angles) * factor], axis=1)
    weight = jnp.where(ks == 32, 1.0, 2.0)[:, None, :, None]
    table = table.astype(BF16)
    return table.reshape(64, SPECTRA), (table * weight.astype(BF16)).reshape(4, 16, SPECTRA)


def prefilter_kernel(v_ref, w_ref, o_ref):
    for s in range(4):
        total = None
        for at in range(s + 1):
            frame = v_ref[:, at * NFFT : (at + 1) * NFFT].astype(F32)
            tap = at - s + 3
            term = w_ref[tap : tap + 1, :] * frame
            total = term if total is None else total + term
        o_ref[s] = total


def prefilter(voltages, window):
    return pl.pallas_call(
        prefilter_kernel,
        in_specs=[VMEM, VMEM],
        out_specs=VMEM,
        out_shape=jax.ShapeDtypeStruct((4, 64, NFFT), F32),
        compiler_params=LEAN,
        name="prefilter",
    )(voltages, window)


def channelize_kernel(p_ref, h_ref, w_ref, t_ref, o_ref, x_ref):
    for s in range(4):
        total = p_ref[s]
        for at in range(s - 3, 0):
            tap = at - s + 3
            total = total + w_ref[tap : tap + 1, :] * h_ref[:, (at + 3) * NFFT : (at + 4) * NFFT].astype(F32)
        low, high = total[:, :HALF], total[:, HALF:]
        x_ref[0, s * 64 : (s + 1) * 64, :] = (low + high).astype(BF16)
        x_ref[1, s * 64 : (s + 1) * 64, :] = (low - high).astype(BF16)

    upper = iota((32, 8, 128), 1) < 4

    def transform(i, _):
        acc = lax.dot_general(t_ref[i], x_ref[i // 4], NT, preferred_element_type=F32)
        first = acc[:, :128].reshape(32, 8, 128)
        second = acc[:, 128:].reshape(32, 8, 128)
        at = pl.ds(pl.multiple_of(i * 32, 32), 32)
        o_ref[at, 0] = jnp.where(upper, first, pltpu.roll(second, 4, 1)).astype(BF16)
        o_ref[at, 1] = jnp.where(upper, pltpu.roll(first, 4, 1), second).astype(BF16)
        return 0

    lax.fori_loop(0, 8, transform, 0)


def channelize(partial_sums, halo, window, table):
    out = pl.pallas_call(
        channelize_kernel,
        in_specs=[VMEM] * 4,
        out_specs=VMEM,
        out_shape=jax.ShapeDtypeStruct((256, 2, 8, 128), BF16),
        scratch_shapes=[pltpu.VMEM((2, 256, HALF), BF16)],
        compiler_params=LEAN,
        name="channelize",
    )(partial_sums, halo, window, table.reshape(8, 256, HALF))
    return out.reshape(512, 8, 128)


def select_kernel(slot_ref, o_ref):
    slots = slot_ref[pl.ds(pl.program_id(0), 1), :]

    def rows(j, _):
        at = pl.ds(pl.multiple_of(j * 256, 256), 256)
        feed = iota((256, 256), 0) + j * 256
        o_ref[0, at, :] = jnp.where(feed == slots, 1.0, 0.0).astype(BF16)
        return 0

    lax.fori_loop(0, 8, rows, 0)


def selection(slots):
    return pl.pallas_call(
        select_kernel,
        grid=(8,),
        in_specs=[VMEM],
        out_specs=pl.BlockSpec((1, 2048, 256), lambda i: (i, 0, 0)),
        out_shape=pltpu.HBM((8, 2048, 256), BF16),
        compiler_params=LEAN,
        name="selection",
    )(slots)


def beam_kernel(r_ref, select_ref, ns_ref, ew_ref, time_ref, o_ref, x_ref, y_ref, z_ref, s_ref):
    @pl.when(pl.program_id(0) == 0)
    def _():
        left = iota((128, 128), 1) < 64

        def assemble(g, _):
            first = r_ref[:, 2 * g].astype(F32).reshape(128, 128)
            second = r_ref[:, 2 * g + 1].astype(F32).reshape(128, 128)
            lanes = pl.ds(pl.multiple_of(g * 128, 128), 128)
            z_ref[0:128, lanes] = jnp.where(left, first, pltpu.roll(second, 64, 1)).astype(BF16)
            z_ref[128:256, lanes] = jnp.where(left, pltpu.roll(first, 64, 1), second).astype(BF16)
            return 0

        lax.fori_loop(0, 16, assemble, 0)
        row = iota((256, 256), 0)
        time = row % 64
        source = (time % 2) * 128 + (time // 4) * 8 + ((time // 2) % 2) * 4 + row // 64
        order = jnp.where(source == iota((256, 256), 1), 1.0, 0.0).astype(BF16)
        x_ref[...] = jnp.dot(order, z_ref[...], preferred_element_type=F32).astype(BF16)

    cp = pl.program_id(0)
    grid = jnp.dot(x_ref[...], select_ref[0], preferred_element_type=F32).astype(BF16)
    for c in range(2):
        both = jnp.dot(grid[c * 128 : (c + 1) * 128], ns_ref[c], preferred_element_type=F32)
        y_ref[c, cp, 0] = both[:64, :256] - both[64:, 256:]
        y_ref[c, cp, 1] = both[64:, :256] + both[:64, 256:]

    @pl.when(pl.program_id(0) == 7)
    def _():
        quarter = iota((16, 128), 1) // 32
        for c in range(2):

            def east(e, _):
                power = None
                for pol in range(2):
                    real, imag = None, None
                    for cyl in range(4):
                        w_re = ew_ref[0, c * 16 + e * 4 + cyl]
                        w_im = ew_ref[1, c * 16 + e * 4 + cyl]
                        y_re = y_ref[c, 2 * cyl + pol, 0]
                        y_im = y_ref[c, 2 * cyl + pol, 1]
                        re = w_re * y_re - w_im * y_im
                        im = w_re * y_im + w_im * y_re
                        real = re if real is None else real + re
                        imag = im if imag is None else imag + im
                    part = real * real + imag * imag
                    power = part if power is None else power + part
                freq = jnp.dot(time_ref[...], power.astype(BF16), preferred_element_type=F32)
                freq = freq.reshape(4, 16, 256)
                for half in range(2):
                    part = freq[:, :, half * 128 : (half + 1) * 128]
                    turned = [part] + [pltpu.roll(part, 32 * n, 2) for n in range(1, 4)]
                    for low in range(4):
                        rows = turned[-low % 4][0]
                        for q in range(1, 4):
                            rows = jnp.where(quarter == q, turned[(q - low) % 4][q], rows)
                        s_ref[pl.ds(e * 16 + (half * 4 + low) * 2 + c, 16, stride=64), :] = rows
                return 0

            lax.fori_loop(0, 4, east, 0)
        o_ref[...] = s_ref[...].astype(BF16)


def form_beams(received, select, ns_table, ew_table, time_table):
    return pl.pallas_call(
        beam_kernel,
        grid=(8,),
        in_specs=[VMEM, pl.BlockSpec((1, 2048, 256), lambda i: (i, 0, 0)), VMEM, SMEM, VMEM],
        out_specs=VMEM,
        out_shape=jax.ShapeDtypeStruct((1024, 128), BF16),
        scratch_shapes=[
            pltpu.VMEM((256, 2048), BF16),
            pltpu.VMEM((2, 8, 2, 64, 256), F32),
            pltpu.VMEM((256, 2048), BF16),
            pltpu.VMEM((1024, 128), F32),
        ],
        compiler_params=LEAN,
        name="beams",
    )(received, select, ns_table, ew_table, time_table)


def phase_kernel(num_ref, d_ref, lut_ref, o_ref):
    first_k = num_ref[0]
    plain = num_ref[1].astype(F32)
    scale = 1.0 - plain
    cos_lut = jnp.broadcast_to(lut_ref[0:1, :], (64, 128))
    sin_lut = jnp.broadcast_to(lut_ref[1:2, :], (64, 128))
    for parity in range(2):

        def fill(i, _):
            at = pl.ds(pl.multiple_of(parity * 512 + i * 64, 64), 64)
            delays = d_ref[pl.ds(i * 128 + parity, 64, stride=2), :]
            turn = (first_k * delays) & (SPECTRA - 1)
            cos = jnp.take_along_axis(cos_lut, turn, axis=1)
            sin = jnp.take_along_axis(sin_lut, turn, axis=1)
            sign = (1 - 2 * (delays & 1)).astype(F32)
            o_ref[0, at, :128] = cos.astype(BF16)
            o_ref[0, at, 128:] = sin.astype(BF16)
            o_ref[1, at, :128] = (sign * (plain + scale * cos)).astype(BF16)
            o_ref[1, at, 128:] = (-scale * sign * sin).astype(BF16)
            return 0

        lax.fori_loop(0, 8, fill, 0)


def phase_tables(numbers, delays, lut):
    return pl.pallas_call(
        phase_kernel,
        grid=(4,),
        in_specs=[SMEM, pl.BlockSpec((CHANS, 128), lambda i: (0, i)), pl.BlockSpec((8, 128), lambda i: (0, 0))],
        out_specs=pl.BlockSpec((2, CHANS, 256), lambda i: (0, 0, i)),
        out_shape=pltpu.HBM((2, CHANS, 1024), BF16),
        compiler_params=LEAN,
        name="phases",
    )(numbers, delays, lut)


def search_kernel(f_ref, t_ref, o_ref, ft_ref):
    @pl.when(pl.program_id(0) == 0)
    def _():
        ft_ref[...] = f_ref[...].astype(F32).T.astype(BF16)

    moved = []
    for pair in range(2):
        both = jnp.dot(ft_ref[pair * 64 : (pair + 1) * 64], t_ref[pair], preferred_element_type=F32)
        moved.append(both[:32, :128] - both[32:, 128:])
        moved.append(both[:32, 128:] + both[32:, :128])
    moved = jnp.concatenate(moved, axis=0) * (1.0 / math.sqrt(CHANS))
    o_ref[...] = moved.T.astype(BF16)


def search(freq, tables):
    return pl.pallas_call(
        search_kernel,
        grid=(4,),
        in_specs=[VMEM, pl.BlockSpec((2, CHANS, 256), lambda i: (0, 0, i))],
        out_specs=pl.BlockSpec((128, 128), lambda i: (i, 0)),
        out_shape=jax.ShapeDtypeStruct((512, 128), BF16),
        scratch_shapes=[pltpu.VMEM((128, CHANS), BF16)],
        compiler_params=LEAN,
        name="search",
    )(freq, tables)


def local(voltages, feed_at_grid_slot, ew_grid, ns_grid, delays):
    tm = lax.axis_index("tm")
    me = tm * 32 + lax.axis_index("feed")
    everyone = ("tm", "feed")
    tail = voltages[:, NFFT:].astype(BF16)
    halo = lax.ppermute(tail, "tm", [(i, i + 1) for i in range(15)])
    window = pfb_window() * (1.0 / 64.0)
    spectra = channelize(prefilter(voltages, window), halo, window, twiddle_tables())
    received = lax.all_to_all(spectra, everyone, split_axis=0, concat_axis=0, tiled=True)

    chan_ids = (me % 256) * 4 + me // 256 + 2 * jnp.arange(2, dtype=jnp.int32) + CHANS
    ew = steer_seed(jnp.arange(4, dtype=jnp.int32), ew_grid, chan_ids, 0.5)
    ew = jnp.stack([x.astype(BF16).astype(F32).transpose(0, 2, 1).reshape(32) for x in ew])
    slots = feed_at_grid_slot.reshape(ROWS, 8).T
    forward, backward = time_rows()
    angles = jnp.arange(128, dtype=jnp.int32) % SPECTRA
    angles = angles.astype(F32) * (TWO_PI / SPECTRA)
    lut = jnp.stack([jnp.cos(angles), jnp.sin(angles)] + [jnp.zeros_like(angles)] * 6)
    numbers = jnp.stack([tm + 1, jnp.where(tm == 15, 1, 0)]).astype(jnp.int32)
    tables = phase_tables(numbers, delays, lut)
    received, tables = lax.optimization_barrier((received, tables))
    tables = pltpu.with_memory_space_constraint(tables, pltpu.HBM)
    select = pltpu.with_memory_space_constraint(selection(slots), pltpu.HBM)
    freq = form_beams(
        received.reshape(16, 32, 8, 128), select, north_tables(ns_grid, chan_ids), ew, forward
    )
    by_freq = lax.all_to_all(freq.reshape(512, 2, 128), everyone, split_axis=0, concat_axis=0, tiled=True)
    moved = search(by_freq.reshape(CHANS, 128), tables)
    combined = lax.all_to_all(moved.reshape(16, 32, 128), "tm", split_axis=0, concat_axis=0, tiled=True)
    combined = combined.reshape(16, 32, 4, 32)
    return jnp.einsum("gdqb,qgt->dbt", combined, backward, preferred_element_type=F32)


def solution(mesh):
    in_specs = (P("feed", "tm"), P(), P(), P(), P())
    out_specs = P("tm", "feed", None)
    return jax.shard_map(local, mesh=mesh, in_specs=in_specs, out_specs=out_specs, check_vma=False)
```

time: 151 us -> 144 us (0.954)
  waiting for transfers between devices: 62.3 us -> 32.1 us
  blocking collectives: 0 us -> 25.9 us
  Pallas kernels: 25.4 us -> 38.1 us
  starting transfers between devices: 43.5 us -> 35.1 us
  local copies, waits for them, and re-layouts: 5.96 us -> 2.25 us
  other arithmetic: 11.2 us -> 8.09 us
    all_to_all x0 -> x1, blocking collectives: none -> 25.9 us  [local(): lax.all_to_all(freq.reshape(512, 2, 128), everyone, split_axis=0, concat_...]
    all_to_all x1 -> x0, waiting for transfers between devices: 15.7 us -> none  [local(): lax.all_to_all(freq, everyone, split_axis=0, concat_axis=0, tiled=True)]
    all_to_all x1, waiting for transfers between devices: 32.3 us -> 17.5 us  [local(): lax.all_to_all(spectra, everyone, split_axis=0, concat_axis=0, tiled=True)]
    pallas_call x3 -> x6, Pallas kernels: 25.4 us -> 38.1 us  [the longest x1 14 us: form_beams(): pl.pallas_call(beam_kernel, grid=(8,), in_specs=[VMEM, pl.BlockSpec((1, 2...]
    all_to_all x1 -> x0, starting transfers between devices: 8.38 us -> none  [local(): lax.all_to_all(freq, everyone, split_axis=0, concat_axis=0, tiled=True)]
    convert_element_type x1, other arithmetic: 3.51 us -> 1.51 us  [twiddle_tables(): return table.astype(BF16).reshape(2, 1024, HALF)]
    reshape x2 -> x0, local copies, waits for them, and re-layouts: 1.67 us -> none  [local(): freq.reshape(2, 4, 4, 16, 8, 32).transpose(3, 1, 4, 0, 2, 5)]
  transfers between devices with their start and end apart: 4 -> 3, of which waited for: 4 -> 3; matrix products, arithmetic and copies ran while one was open for 7% -> 5% of each run, Pallas kernels for 0% -> 11%
where the time goes in v2:
time: 144 us; the launch traced here: 143 us
  Pallas kernels  38.1 us (26%)
  starting transfers between devices  35.1 us (24%)
  waiting for transfers between devices  32.1 us (22%)
  blocking collectives  25.9 us (18%)
  other arithmetic  8.09 us (6%)
  local copies, waits for them, and re-layouts  2.25 us (2%)
    all_to_all x1, starting transfers between devices, local(): lax.all_to_all(spectra, everyone, split_axis=0, concat_axis=0, tiled=True)  26.8 us
    all_to_all x1, blocking collectives, local(): lax.all_to_all(freq.reshape(512, 2, 128), everyone, split_axis=0, concat_...  25.9 us
    all_to_all x1, waiting for transfers between devices, local(): lax.all_to_all(spectra, everyone, split_axis=0, concat_axis=0, tiled=True)  17.5 us
    pallas_call x1, Pallas kernels, form_beams(): pl.pallas_call(beam_kernel, grid=(8,), in_specs=[VMEM, pl.BlockSpec((1, 2...  14 us
    pallas_call x1, Pallas kernels, phase_tables(): pl.pallas_call(phase_kernel, grid=(4,), in_specs=[SMEM, pl.BlockSpec((CHA...  9.23 us
    all_to_all x1, waiting for transfers between devices, local(): lax.all_to_all(moved.reshape(16, 32, 128), 'tm', split_axis=0, concat_axi...  8.79 us
    ppermute x1, waiting for transfers between devices, local(): halo = lax.ppermute(tail, 'tm', [(i, i + 1) for i in range(15)])  5.88 us
    pallas_call x1, Pallas kernels, selection(): pl.pallas_call(select_kernel, grid=(8,), in_specs=[VMEM], out_specs=pl.Bl...  5.5 us
  transfers between devices with their start and end apart: 3, of which 3 were waited for; matrix products, arithmetic and copies ran while one was open for 5% of the time, Pallas kernels for 11%

profile of v2, /device:TPU:1, one launch (start us, length us, event | category | flops | bytes accessed | tf_op | source)
XLA Modules:
  0.0 143.1 jit_solution(14716280709459283112)
XLA Ops:
  0.0 1.5 %slice_convert_fusion = bf16[64,6144]{1,0:T(8,128)(2,1)S(1)} fusion(s32[64,8192]{1,0:T(8,128)} %v_ref.1), kind=kLoop, calls=%fused_computation.1 | loop fusion | flops 393216 | bytes 2359296 | tf_op jit(solution)/shard_map/convert.1
  1.5 4.9 %collective-permute-start = (bf16[64,6144]{1,0:T(8,128)(2,1)S(1)}, bf16[64,6144]{1,0:T(8,128)(2,1)S(1)}, u32[]{:S(2)}, u32[]{:S(2)}) collective-permute-start(bf16[64,6144]{1,0:T(8,128)(2,1)S(1)} %slice_convert_fusion), channel_id=1, source_target_pairs={{0,32},{32,64},{64,96},{96,128},{128,160},{160,192},{192,224},{224... | collective-permute-start | bytes 2359304 | tf_op jit(solution)/shard_map/ppermute | solution.py:317
  6.4 0.5 fusion.10
  7.0 0.4 multiply_reduce_fusion
  7.4 0.8 iota_multiply_fusion
  8.1 0.3 sine_multiply_fusion.1
  8.5 0.3 divide_multiply_fusion.w_ref
  8.8 1.1 sine_multiply_fusion
  10.0 1.6 %copy-done = s32[64,8192]{1,0:T(8,128)S(1)} copy-done((s32[64,8192]{1,0:T(8,128)S(1)}, s32[64,8192]{1,0:T(8,128)}, u32[]{:S(2)}) %copy-start) | copy-done | bytes 2097176
  11.6 0.5 prefilter.1.p_ref
  12.0 0.7 iota_multiply_fusion.1
  12.8 1.5 %subtract_convert_fusion = bf16[2,32,32,1024]{3,2,1,0:T(8,128)(2,1)S(1)} fusion(f32[2,32,1024]{2,1,0:T(8,128)S(1)} %get-tuple-element.18, f32[32,1024]{1,0:T(8,128)S(1)} %get-tuple-element.17, f32[2,32,1024]{2,1,0:T(8,128)S(1)} %get-tuple-element.16, f32[32,1024]{1,0:T(8,128)S(1)} %get-tuple-element.15), kind=kLoop, calls=%fused_computation | loop fusion | flops 8388608 | bytes 4980736 | tf_op jit(solution)/shard_map/convert_element_type | solution.py:53
  14.3 5.9 %collective-permute-done.h_ref = bf16[64,6144]{1,0:T(8,128)(2,1)S(1)} collective-permute-done((bf16[64,6144]{1,0:T(8,128)(2,1)S(1)}, bf16[64,6144]{1,0:T(8,128)(2,1)S(1)}, u32[]{:S(2)}, u32[]{:S(2)}) %collective-permute-start) | collective-permute-done | bytes 786464 | tf_op jit(solution)/shard_map/ppermute | solution.py:317
  20.2 4.2 %channelize.1 = bf16[256,2,8,128]{3,2,1,0:T(8,128)(2,1)} custom-call(f32[4,64,2048]{2,1,0:T(8,128)S(1)} %prefilter.1.p_ref, bf16[64,6144]{1,0:T(8,128)(2,1)S(1)} %collective-permute-done.h_ref, f32[4,2048]{1,0:T(4,128)S(1)} %divide_multiply_fusion.w_ref, bf16[8,256,1024]{2,1,0:T(8,128)(2,1)S(1)} %bitcast.21), custom_call_target="tpu_custom_call" | custom-call | tf_op jit(solution)/shard_map/channelize/pallas_call | solution.py:132
  24.4 26.8 %all-to-all-start = ((bf16[512,8,128]{2,1,0:T(8,128)(2,1)}), bf16[512,8,128]{2,1,0:T(8,128)(2,1)S(1)}, u32[]{:S(2)}, u32[]{:S(2)}) async-start(bf16[512,8,128]{2,1,0:T(8,128)(2,1)} %bitcast.1), calls=%async_computation | async-start | bytes 2097152 | tf_op jit(solution)/shard_map/all_to_all | solution.py:320
  51.2 0.1 mul.569
  51.3 0.1 pad.10.clone
  51.4 0.1 pad.11.clone
  51.5 0.1 reshape.391
  51.7 5.5 %selection.1.select_ref = bf16[8,2048,256]{2,1,0:T(8,128)(2,1)} custom-call(s32[8,256]{1,0:T(8,128)S(1)} %bitcast.26), custom_call_target="tpu_custom_call" | custom-call | tf_op jit(solution)/shard_map/selection/pallas_call | solution.py:157
  57.4 9.2 %phases.1.t_ref = bf16[2,1024,1024]{2,1,0:T(8,128)(2,1)} custom-call(s32[2]{0:T(128)S(1)} %pad_add_fusion.1.num_ref, s32[1024,512]{1,0:T(8,128)S(1)} %copy-done.1, f32[8,128]{1,0:T(8,128)S(1)} %maximum_maximum_fusion.lut_ref), custom_call_target="tpu_custom_call" | custom-call | tf_op jit(solution)/shard_map/phases/pallas_call | solution.py:274
  66.7 0.2 cosine_multiply_fusion.2
  66.9 0.2 subtract_convert_fusion.1
  67.1 17.5 %all-to-all-done = bf16[512,8,128]{2,1,0:T(8,128)(2,1)S(1)} async-done(((bf16[512,8,128]{2,1,0:T(8,128)(2,1)}), bf16[512,8,128]{2,1,0:T(8,128)(2,1)S(1)}, u32[]{:S(2)}, u32[]{:S(2)}) %all-to-all-start) | async-done | bytes 1048608 | tf_op jit(solution)/shard_map/all_to_all | solution.py:320
  84.6 14.0 %beams.1 = bf16[1024,128]{1,0:T(8,128)(2,1)S(1)} custom-call(bf16[16,32,8,128]{3,2,1,0:T(8,128)(2,1)S(1)} %bitcast.22, bf16[8,2048,256]{2,1,0:T(8,128)(2,1)} %selection.1.select_ref, bf16[2,256,512]{2,1,0:T(8,128)(2,1)S(1)} %pad_maximum_fusion.ns_ref, f32[2,32]{1,0:T(2,128)S(1)} %maximum_convert_fusion.1.ew_ref, bf16[64,64]{1,0:T(8,128)(2,1)S(1)} %bitcast.25), custom_call_target="tpu_custom_call" | custom-call | tf_op jit(solution)/shard_map/beams/pallas_call | solution.py:232
  98.6 25.9 %all_to_all.15 = bf16[512,2,128]{2,1,0:T(2,128)(2,1)S(1)} all-to-all(bf16[512,2,128]{2,1,0:T(2,128)(2,1)S(1)} %bitcast.24), channel_id=1, replica_groups=mesh['tm'=16,'feed'=32] {'tm','feed'}, dimensions={0} | all-to-all | bytes 524288 | tf_op jit(solution)/shard_map/all_to_all | solution.py:338
  124.5 4.7 %search.1 = bf16[512,128]{1,0:T(8,128)(2,1)} custom-call(bf16[1024,128]{1,0:T(8,128)(2,1)S(1)} %bitcast.23, bf16[2,1024,1024]{2,1,0:T(8,128)(2,1)} %phases.1.t_ref), custom_call_target="tpu_custom_call" | custom-call | tf_op jit(solution)/shard_map/search/pallas_call | solution.py:300
  129.1 3.5 %all-to-all-start.2 = ((bf16[16,32,128]{2,1,0:T(8,128)(2,1)}), bf16[16,32,128]{2,1,0:T(8,128)(2,1)S(1)}, u32[]{:S(2)}, u32[]{:S(2)}) async-start(bf16[16,32,128]{2,1,0:T(8,128)(2,1)} %bitcast.11), calls=%async_computation.2 | async-start | bytes 262144 | tf_op jit(solution)/shard_map/all_to_all | solution.py:340
  132.7 0.1 bitcast_multiply_fusion
  132.8 8.8 %all-to-all-done.2 = bf16[16,32,128]{2,1,0:T(8,128)(2,1)S(1)} async-done(((bf16[16,32,128]{2,1,0:T(8,128)(2,1)}), bf16[16,32,128]{2,1,0:T(8,128)(2,1)S(1)}, u32[]{:S(2)}, u32[]{:S(2)}) %all-to-all-start.2) | async-done | bytes 131104 | tf_op jit(solution)/shard_map/all_to_all | solution.py:340
  141.6 0.2 reshape.395
  141.8 1.3 convolution_bitcast_fusion
  (27 shorter events, 0.6 us)
Async XLA Ops:
  1.5 18.7 %collective-permute-start = (bf16[64,6144]{1,0:T(8,128)(2,1)S(1)}, bf16[64,6144]{1,0:T(8,128)(2,1)S(1)}, u32[]{:S(2)}, u32[]{:S(2)}) collective-permute-start(bf16[64,6144]{1,0:T(8,128)(2,1)S(1)} %slice_convert_fusion), channel_id=1, source_target_pairs={{0,32},{32,64},{64,96},{96,128},{128,160},{160,192},{192,224},{224... | collective-permute-start | bytes 2359304 | tf_op jit(solution)/shard_map/ppermute | solution.py:317
  10.0 1.6 %copy-start = (s32[64,8192]{1,0:T(8,128)S(1)}, s32[64,8192]{1,0:T(8,128)}, u32[]{:S(2)}) copy-start(s32[64,8192]{1,0:T(8,128)} %v_ref.1) | copy-start | bytes 6291460
  12.0 39.5 %copy-start.2 = (s32[2048]{0:T(1024)S(1)}, s32[2048]{0:T(1024)}, u32[]{:S(2)}) copy-start(s32[2048]{0:T(1024)} %param.6) | copy-start | bytes 24580
  20.2 37.2 %copy-start.1 = (s32[1024,512]{1,0:T(8,128)S(1)}, s32[1024,512]{1,0:T(8,128)}, u32[]{:S(2)}) copy-start(s32[1024,512]{1,0:T(8,128)} %d_ref.1) | copy-start | bytes 6291460
  24.4 60.2 %all-to-all-start = ((bf16[512,8,128]{2,1,0:T(8,128)(2,1)}), bf16[512,8,128]{2,1,0:T(8,128)(2,1)S(1)}, u32[]{:S(2)}, u32[]{:S(2)}) async-start(bf16[512,8,128]{2,1,0:T(8,128)(2,1)} %bitcast.1), calls=%async_computation | async-start | bytes 2097152 | tf_op jit(solution)/shard_map/all_to_all | solution.py:320
  129.1 12.4 %all-to-all-start.2 = ((bf16[16,32,128]{2,1,0:T(8,128)(2,1)}), bf16[16,32,128]{2,1,0:T(8,128)(2,1)S(1)}, u32[]{:S(2)}, u32[]{:S(2)}) async-start(bf16[16,32,128]{2,1,0:T(8,128)(2,1)} %bitcast.11), calls=%async_computation.2 | async-start | bytes 262144 | tf_op jit(solution)/shard_map/all_to_all | solution.py:340

commit v3 on v2

--- a/solution.py
+++ b/solution.py
@@ -6,7 +6,7 @@
 from jax import lax
 from jax.experimental import pallas as pl
 from jax.experimental.pallas import tpu as pltpu
-from jax.sharding import PartitionSpec as P
+from jax.sharding import Mesh, PartitionSpec as P
 
 NFFT = 2048
 CHANS = 1024
@@ -17,6 +17,8 @@
 TWO_PI = 2.0 * math.pi
 PHASE_MODULUS = 1048576
 F32 = jnp.float32
+TIME = ("y", "z_lo")
+FEED = ("z_hi", "x", "core")
 BF16 = jnp.bfloat16
 NT = (((1,), (1,)), ((), ()))
 
@@ -79,65 +81,108 @@
     table = jnp.stack([jnp.cos(angles) * factor, -jnp.sin(angles) * factor], axis=1)
     weight = jnp.where(ks == 32, 1.0, 2.0)[:, None, :, None]
     table = table.astype(BF16)
-    return table.reshape(64, SPECTRA), (table * weight.astype(BF16)).reshape(4, 16, SPECTRA)
-
-
-def prefilter_kernel(v_ref, w_ref, o_ref):
-    for s in range(4):
+    return jnp.roll(table, -1, axis=-1).reshape(64, SPECTRA), (table * weight.astype(BF16)).reshape(4, 16, SPECTRA)
+
+
+def prefilter_kernel(keep_ref, v_ref, w_ref, o_ref):
+    for s in range(1, 5):
         total = None
-        for at in range(s + 1):
+        for at in range(max(0, s - 3), min(4, s + 1)):
             frame = v_ref[:, at * NFFT : (at + 1) * NFFT].astype(F32)
             tap = at - s + 3
             term = w_ref[tap : tap + 1, :] * frame
             total = term if total is None else total + term
-        o_ref[s] = total
-
-
-def prefilter(voltages, window):
+        o_ref[s - 1] = total if s < 4 else jnp.where(keep_ref[0] == 1, total, 0.0)
+
+
+def in_hbm(x):
+    return pltpu.with_memory_space_constraint(x, pltpu.HBM)
+
+
+def whole(shape):
+    return pl.BlockSpec(shape, lambda i: (0, 0))
+
+
+def edges_kernel(v_ref, back_ref, ahead_ref):
+    frame = v_ref[...].astype(BF16)
+
+    @pl.when(pl.program_id(0) < 2)
+    def _():
+        back_ref[...] = frame
+
+    @pl.when(pl.program_id(0) == 2)
+    def _():
+        ahead_ref[...] = frame
+
+
+def edges(voltages):
+    return pl.pallas_call(
+        edges_kernel,
+        grid=(3,),
+        in_specs=[pl.BlockSpec((64, NFFT), lambda i: (0, (i + 2) % 4))],
+        out_specs=[pl.BlockSpec((64, NFFT), lambda i: (0, jnp.minimum(i, 1))), whole((64, NFFT))],
+        out_shape=[jax.ShapeDtypeStruct((64, 2 * NFFT), BF16), jax.ShapeDtypeStruct((64, NFFT), BF16)],
+        compiler_params=LEAN,
+        name="edges",
+    )(voltages)
+
+
+def prefilter(keep, voltages, window):
     return pl.pallas_call(
         prefilter_kernel,
-        in_specs=[VMEM, VMEM],
+        in_specs=[SMEM, VMEM, VMEM],
         out_specs=VMEM,
         out_shape=jax.ShapeDtypeStruct((4, 64, NFFT), F32),
         compiler_params=LEAN,
         name="prefilter",
-    )(voltages, window)
-
-
-def channelize_kernel(p_ref, h_ref, w_ref, t_ref, o_ref, x_ref):
-    for s in range(4):
-        total = p_ref[s]
-        for at in range(s - 3, 0):
-            tap = at - s + 3
-            total = total + w_ref[tap : tap + 1, :] * h_ref[:, (at + 3) * NFFT : (at + 4) * NFFT].astype(F32)
-        low, high = total[:, :HALF], total[:, HALF:]
-        x_ref[0, s * 64 : (s + 1) * 64, :] = (low + high).astype(BF16)
-        x_ref[1, s * 64 : (s + 1) * 64, :] = (low - high).astype(BF16)
-
-    upper = iota((32, 8, 128), 1) < 4
-
-    def transform(i, _):
-        acc = lax.dot_general(t_ref[i], x_ref[i // 4], NT, preferred_element_type=F32)
-        first = acc[:, :128].reshape(32, 8, 128)
-        second = acc[:, 128:].reshape(32, 8, 128)
-        at = pl.ds(pl.multiple_of(i * 32, 32), 32)
-        o_ref[at, 0] = jnp.where(upper, first, pltpu.roll(second, 4, 1)).astype(BF16)
-        o_ref[at, 1] = jnp.where(upper, pltpu.roll(first, 4, 1), second).astype(BF16)
-        return 0
-
-    lax.fori_loop(0, 8, transform, 0)
-
-
-def channelize(partial_sums, halo, window, table):
+    )(keep, voltages, window)
+
+
+def channelize_kernel(p_ref, back_ref, ahead_ref, w_ref, t_ref, o_ref, x_ref):
+    @pl.when(pl.program_id(0) == 0)
+    def _():
+        def filter_rows(i, _):
+            at = pl.ds(pl.multiple_of(i * 16, 16), 16)
+
+            def term(tap, ref, frame):
+                return w_ref[tap : tap + 1, :] * ref[at, frame * NFFT : (frame + 1) * NFFT].astype(F32)
+
+            for s in range(4):
+                total = p_ref[s, at, :]
+                if s == 0:
+                    total = total + term(0, back_ref, 0) + term(1, back_ref, 1)
+                elif s == 1:
+                    total = total + term(0, back_ref, 1)
+                elif s == 3:
+                    total = total + term(3, ahead_ref, 0)
+                low, high = total[:, :HALF], total[:, HALF:]
+                to = pl.ds(pl.multiple_of(s * 64 + i * 16, 16), 16)
+                x_ref[0, to, :] = (low + high).astype(BF16)
+                x_ref[1, to, :] = (low - high).astype(BF16)
+            return 0
+
+        lax.fori_loop(0, 4, filter_rows, 0)
+
+    upper = iota((64, 8, 128), 1) < 4
+    acc = lax.dot_general(t_ref[...], x_ref[pl.program_id(0) // 2], NT, preferred_element_type=F32)
+    first = acc[:, :128].reshape(64, 8, 128)
+    second = acc[:, 128:].reshape(64, 8, 128)
+    o_ref[:, 0] = jnp.where(upper, first, pltpu.roll(second, 4, 1)).astype(BF16)
+    o_ref[:, 1] = jnp.where(upper, pltpu.roll(first, 4, 1), second).astype(BF16)
+
+
+def channelize(partial_sums, back, ahead, window, table):
     out = pl.pallas_call(
         channelize_kernel,
-        in_specs=[VMEM] * 4,
-        out_specs=VMEM,
+        grid=(4,),
+        in_specs=[VMEM, whole((64, 2 * NFFT)), whole((64, NFFT)), VMEM]
+        + [pl.BlockSpec((512, HALF), lambda i: (i, 0))],
+        out_specs=pl.BlockSpec((64, 2, 8, 128), lambda i: (i, 0, 0, 0)),
         out_shape=jax.ShapeDtypeStruct((256, 2, 8, 128), BF16),
         scratch_shapes=[pltpu.VMEM((2, 256, HALF), BF16)],
         compiler_params=LEAN,
         name="channelize",
-    )(partial_sums, halo, window, table.reshape(8, 256, HALF))
+    )(partial_sums, in_hbm(back), in_hbm(ahead), window, in_hbm(table.reshape(2048, HALF)))
     return out.reshape(512, 8, 128)
 
 
@@ -171,8 +216,8 @@
         left = iota((128, 128), 1) < 64
 
         def assemble(g, _):
-            first = r_ref[:, 2 * g].astype(F32).reshape(128, 128)
-            second = r_ref[:, 2 * g + 1].astype(F32).reshape(128, 128)
+            first = r_ref[0, g // 4, :, g % 4].astype(F32).reshape(128, 128)
+            second = r_ref[1, g // 4, :, g % 4].astype(F32).reshape(128, 128)
             lanes = pl.ds(pl.multiple_of(g * 128, 128), 128)
             z_ref[0:128, lanes] = jnp.where(left, first, pltpu.roll(second, 64, 1)).astype(BF16)
             z_ref[128:256, lanes] = jnp.where(left, pltpu.roll(first, 64, 1), second).astype(BF16)
@@ -181,18 +226,20 @@
         lax.fori_loop(0, 16, assemble, 0)
         row = iota((256, 256), 0)
         time = row % 64
-        source = (time % 2) * 128 + (time // 4) * 8 + ((time // 2) % 2) * 4 + row // 64
+        source = (time % 2) * 128 + ((time // 4) % 2) * 64 + (time // 8) * 8 + ((time // 2) % 2) * 4 + row // 64
         order = jnp.where(source == iota((256, 256), 1), 1.0, 0.0).astype(BF16)
         x_ref[...] = jnp.dot(order, z_ref[...], preferred_element_type=F32).astype(BF16)
 
-    cp = pl.program_id(0)
-    grid = jnp.dot(x_ref[...], select_ref[0], preferred_element_type=F32).astype(BF16)
+    grids = [jnp.dot(x_ref[...], select_ref[pol], preferred_element_type=F32).astype(BF16) for pol in range(2)]
+    cyl = pl.program_id(0)
     for c in range(2):
-        both = jnp.dot(grid[c * 128 : (c + 1) * 128], ns_ref[c], preferred_element_type=F32)
-        y_ref[c, cp, 0] = both[:64, :256] - both[64:, 256:]
-        y_ref[c, cp, 1] = both[64:, :256] + both[:64, 256:]
-
-    @pl.when(pl.program_id(0) == 7)
+        rows = jnp.concatenate([grid[c * 128 : (c + 1) * 128] for grid in grids], axis=0)
+        both = jnp.dot(rows, ns_ref[c], preferred_element_type=F32)
+        for pol in range(2):
+            y_ref[c, cyl, pol, 0] = both[pol * 128 : pol * 128 + 64, :256] - both[pol * 128 + 64 : pol * 128 + 128, 256:]
+            y_ref[c, cyl, pol, 1] = both[pol * 128 + 64 : pol * 128 + 128, :256] + both[pol * 128 : pol * 128 + 64, 256:]
+
+    @pl.when(pl.program_id(0) == 3)
     def _():
         quarter = iota((16, 128), 1) // 32
         for c in range(2):
@@ -200,16 +247,15 @@
             def east(e, _):
                 power = None
                 for pol in range(2):
-                    real, imag = None, None
-                    for cyl in range(4):
+                    real = 0.5 * y_ref[c, 0, pol, 0]
+                    imag = 0.5 * y_ref[c, 0, pol, 1]
+                    for cyl in range(1, 4):
                         w_re = ew_ref[0, c * 16 + e * 4 + cyl]
                         w_im = ew_ref[1, c * 16 + e * 4 + cyl]
-                        y_re = y_ref[c, 2 * cyl + pol, 0]
-                        y_im = y_ref[c, 2 * cyl + pol, 1]
-                        re = w_re * y_re - w_im * y_im
-                        im = w_re * y_im + w_im * y_re
-                        real = re if real is None else real + re
-                        imag = im if imag is None else imag + im
+                        y_re = y_ref[c, cyl, pol, 0]
+                        y_im = y_ref[c, cyl, pol, 1]
+                        real = real + (w_re * y_re - w_im * y_im)
+                        imag = imag + (w_re * y_im + w_im * y_re)
                     part = real * real + imag * imag
                     power = part if power is None else power + part
                 freq = jnp.dot(time_ref[...], power.astype(BF16), preferred_element_type=F32)
@@ -221,7 +267,9 @@
                         rows = turned[-low % 4][0]
                         for q in range(1, 4):
                             rows = jnp.where(quarter == q, turned[(q - low) % 4][q], rows)
-                        s_ref[pl.ds(e * 16 + (half * 4 + low) * 2 + c, 16, stride=64), :] = rows
+                        bh = half * 4 + low
+                        start = ((bh % 2) * 256 + e * 64 + bh // 2) * 2 + c
+                        s_ref[pl.ds(start, 16, stride=8), :] = rows
                 return 0
 
             lax.fori_loop(0, 4, east, 0)
@@ -231,13 +279,13 @@
 def form_beams(received, select, ns_table, ew_table, time_table):
     return pl.pallas_call(
         beam_kernel,
-        grid=(8,),
-        in_specs=[VMEM, pl.BlockSpec((1, 2048, 256), lambda i: (i, 0, 0)), VMEM, SMEM, VMEM],
+        grid=(4,),
+        in_specs=[VMEM, pl.BlockSpec((2, 2048, 256), lambda i: (i, 0, 0)), VMEM, SMEM, VMEM],
         out_specs=VMEM,
         out_shape=jax.ShapeDtypeStruct((1024, 128), BF16),
         scratch_shapes=[
             pltpu.VMEM((256, 2048), BF16),
-            pltpu.VMEM((2, 8, 2, 64, 256), F32),
+            pltpu.VMEM((2, 4, 2, 2, 64, 256), F32),
             pltpu.VMEM((256, 2048), BF16),
             pltpu.VMEM((1024, 128), F32),
         ],
@@ -282,41 +330,42 @@
     )(numbers, delays, lut)
 
 
-def search_kernel(f_ref, t_ref, o_ref, ft_ref):
-    @pl.when(pl.program_id(0) == 0)
-    def _():
-        ft_ref[...] = f_ref[...].astype(F32).T.astype(BF16)
-
-    moved = []
-    for pair in range(2):
-        both = jnp.dot(ft_ref[pair * 64 : (pair + 1) * 64], t_ref[pair], preferred_element_type=F32)
-        moved.append(both[:32, :128] - both[32:, 128:])
-        moved.append(both[:32, 128:] + both[32:, :128])
-    moved = jnp.concatenate(moved, axis=0) * (1.0 / math.sqrt(CHANS))
-    o_ref[...] = moved.T.astype(BF16)
+def search_kernel(f_ref, t_ref, o_ref):
+    freq = f_ref[...].astype(F32).T.astype(BF16)
+    sums = [jnp.dot(freq[pair * 64 : (pair + 1) * 64], t_ref[pair], preferred_element_type=F32) for pair in range(2)]
+    for j in range(4):
+        moved = []
+        for pair in range(2):
+            cos = sums[pair][:, j * 256 : j * 256 + 128]
+            sin = sums[pair][:, j * 256 + 128 : j * 256 + 256]
+            moved.append(cos[:32] - sin[32:])
+            moved.append(sin[:32] + cos[32:])
+        moved = jnp.concatenate(moved, axis=0) * (1.0 / math.sqrt(CHANS))
+        o_ref[j * 128 : (j + 1) * 128, :] = moved.T.astype(BF16)
 
 
 def search(freq, tables):
     return pl.pallas_call(
         search_kernel,
-        grid=(4,),
-        in_specs=[VMEM, pl.BlockSpec((2, CHANS, 256), lambda i: (0, 0, i))],
-        out_specs=pl.BlockSpec((128, 128), lambda i: (i, 0)),
+        in_specs=[VMEM, VMEM],
+        out_specs=VMEM,
         out_shape=jax.ShapeDtypeStruct((512, 128), BF16),
-        scratch_shapes=[pltpu.VMEM((128, CHANS), BF16)],
         compiler_params=LEAN,
         name="search",
     )(freq, tables)
 
 
 def local(voltages, feed_at_grid_slot, ew_grid, ns_grid, delays):
-    tm = lax.axis_index("tm")
-    me = tm * 32 + lax.axis_index("feed")
-    everyone = ("tm", "feed")
-    tail = voltages[:, NFFT:].astype(BF16)
-    halo = lax.ppermute(tail, "tm", [(i, i + 1) for i in range(15)])
+    tm = lax.axis_index(TIME)
+    everyone = ("core", "z_hi", "z_lo", "y", "x")
+    me = lax.axis_index(everyone)
+    block = lax.axis_index(("z_lo", "y"))
+    back, ahead = edges(in_hbm(voltages))
+    back = lax.ppermute(back, TIME, [(i, i + 1) for i in range(15)])
+    ahead = lax.ppermute(ahead, TIME, [((i + 1) % 16, i) for i in range(16)])
     window = pfb_window() * (1.0 / 64.0)
-    spectra = channelize(prefilter(voltages, window), halo, window, twiddle_tables())
+    keep = jnp.where(tm == 15, 0, 1).astype(jnp.int32).reshape(1)
+    spectra = channelize(prefilter(keep, voltages, window), back, ahead, window, twiddle_tables())
     received = lax.all_to_all(spectra, everyone, split_axis=0, concat_axis=0, tiled=True)
 
     chan_ids = (me % 256) * 4 + me // 256 + 2 * jnp.arange(2, dtype=jnp.int32) + CHANS
@@ -327,22 +376,22 @@
     angles = jnp.arange(128, dtype=jnp.int32) % SPECTRA
     angles = angles.astype(F32) * (TWO_PI / SPECTRA)
     lut = jnp.stack([jnp.cos(angles), jnp.sin(angles)] + [jnp.zeros_like(angles)] * 6)
-    numbers = jnp.stack([tm + 1, jnp.where(tm == 15, 1, 0)]).astype(jnp.int32)
+    numbers = jnp.stack([block + 1, jnp.where(block == 15, 1, 0)]).astype(jnp.int32)
     tables = phase_tables(numbers, delays, lut)
     received, tables = lax.optimization_barrier((received, tables))
-    tables = pltpu.with_memory_space_constraint(tables, pltpu.HBM)
     select = pltpu.with_memory_space_constraint(selection(slots), pltpu.HBM)
     freq = form_beams(
-        received.reshape(16, 32, 8, 128), select, north_tables(ns_grid, chan_ids), ew, forward
+        received.reshape(2, 4, 16, 4, 8, 128), select, north_tables(ns_grid, chan_ids), ew, forward
     )
     by_freq = lax.all_to_all(freq.reshape(512, 2, 128), everyone, split_axis=0, concat_axis=0, tiled=True)
     moved = search(by_freq.reshape(CHANS, 128), tables)
-    combined = lax.all_to_all(moved.reshape(16, 32, 128), "tm", split_axis=0, concat_axis=0, tiled=True)
+    combined = lax.all_to_all(moved.reshape(16, 32, 128), TIME, split_axis=0, concat_axis=0, tiled=True)
     combined = combined.reshape(16, 32, 4, 32)
+    backward = backward.reshape(4, 2, 8, SPECTRA).transpose(0, 2, 1, 3).reshape(4, 16, SPECTRA)
     return jnp.einsum("gdqb,qgt->dbt", combined, backward, preferred_element_type=F32)
 
 
 def solution(mesh):
-    in_specs = (P("feed", "tm"), P(), P(), P(), P())
-    out_specs = P("tm", "feed", None)
-    return jax.shard_map(local, mesh=mesh, in_specs=in_specs, out_specs=out_specs, check_vma=False)
+    split = Mesh(mesh.devices.reshape(8, 2, 4, 4, 2), ("y", "z_lo", "z_hi", "x", "core"))
+    in_specs = (P(FEED, TIME), P(), P(), P(), P())
+    return jax.shard_map(local, mesh=split, in_specs=in_specs, out_specs=P(TIME, FEED, None), check_vma=False)

time: 144 us -> 139 us (0.965)
  waiting for transfers between devices: 32.1 us -> 28.6 us
  Pallas kernels: 38.1 us -> 36.3 us
    ppermute x1 -> x2, starting transfers between devices: 4.86 us -> 9.82 us  [the longest x1 7.72 us: local(): ahead = lax.ppermute(ahead, TIME, [((i + 1) % 16, i) for i in range(16)])]
    all_to_all x1, starting transfers between devices: 26.8 us -> 22.8 us  [local(): lax.all_to_all(spectra, everyone, split_axis=0, concat_axis=0, tiled=True)]
    convert_element_type x1, other arithmetic: 1.51 us -> 3.46 us  [twiddle_tables(): return table.astype(BF16).reshape(2, 1024, HALF)]
    pallas_call x4 -> x5, Pallas kernels: 23.4 us -> 21.6 us  [the longest x1 11.4 us: form_beams(): pl.pallas_call(beam_kernel, grid=(4,), in_specs=[VMEM, pl.BlockSpec((2, 2...]
    ppermute x1 -> x2, waiting for transfers between devices: 5.88 us -> 4.19 us  [the longest x1 4.19 us: local(): back = lax.ppermute(back, TIME, [(i, i + 1) for i in range(15)])]
    unnamed x6 -> x10, local copies, waits for them, and re-layouts: 1.6 us -> 0.02 us
    another operation x2 -> x1, other arithmetic: 1.56 us -> 0.07 us  [local(): jnp.stack([block + 1, jnp.where(block == 15, 1, 0)]).astype(jnp.int32)]
    all_to_all x1, waiting for transfers between devices: 17.5 us -> 16 us  [local(): lax.all_to_all(spectra, everyone, split_axis=0, concat_axis=0, tiled=True)]
  transfers between devices with their start and end apart: 3 -> 4, of which waited for: 3 -> 3; matrix products, arithmetic and copies ran while one was open for 5% -> 6% of each run, Pallas kernels for 11% -> 11%
where the time goes in v3:
time: 139 us; the launch traced here: 138 us
  Pallas kernels  36.3 us (26%)
  starting transfers between devices  36.1 us (26%)
  waiting for transfers between devices  28.6 us (21%)
  blocking collectives  26.8 us (19%)
  other arithmetic  7.97 us (6%)
    all_to_all x1, blocking collectives, local(): lax.all_to_all(freq.reshape(512, 2, 128), everyone, split_axis=0, concat_...  26.8 us
    all_to_all x1, starting transfers between devices, local(): lax.all_to_all(spectra, everyone, split_axis=0, concat_axis=0, tiled=True)  22.8 us
    all_to_all x1, waiting for transfers between devices, local(): lax.all_to_all(spectra, everyone, split_axis=0, concat_axis=0, tiled=True)  16 us
    pallas_call x1, Pallas kernels, form_beams(): pl.pallas_call(beam_kernel, grid=(4,), in_specs=[VMEM, pl.BlockSpec((2, 2...  11.4 us
    pallas_call x1, Pallas kernels, phase_tables(): pl.pallas_call(phase_kernel, grid=(4,), in_specs=[SMEM, pl.BlockSpec((CHA...  9.22 us
    all_to_all x1, waiting for transfers between devices, local(): lax.all_to_all(moved.reshape(16, 32, 128), TIME, split_axis=0, concat_axi...  8.39 us
    ppermute x1, starting transfers between devices, local(): ahead = lax.ppermute(ahead, TIME, [((i + 1) % 16, i) for i in range(16)])  7.72 us
    pallas_call x1, Pallas kernels, channelize(): pl.pallas_call(channelize_kernel, grid=(4,), in_specs=[VMEM, whole((64, 2...  5.62 us
  transfers between devices with their start and end apart: 4, of which 3 were waited for; matrix products, arithmetic and copies ran while one was open for 6% of the time, Pallas kernels for 11%

profile of v3, /device:TPU:1, one launch (start us, length us, event | category | flops | bytes accessed | tf_op | source)
XLA Modules:
  0.0 138.2 jit_solution(8811115401991621328)
XLA Ops:
  0.0 2.5 %edges.1 = (bf16[64,4096]{1,0:T(8,128)(2,1)S(1)}, bf16[64,2048]{1,0:T(8,128)(2,1)S(1)}) custom-call(s32[64,8192]{1,0:T(8,128)} %v_ref.3), custom_call_target="tpu_custom_call" | custom-call | tf_op jit(solution)/shard_map/edges/pallas_call | solution.py:119
  2.5 7.7 %collective-permute-start.1 = (bf16[64,2048]{1,0:T(8,128)(2,1)S(1)}, bf16[64,2048]{1,0:T(8,128)(2,1)}, u32[]{:S(2)}, u32[]{:S(2)}) collective-permute-start(bf16[64,2048]{1,0:T(8,128)(2,1)S(1)} %get-tuple-element.18), channel_id=1, source_target_pairs={{32,0},{64,32},{96,64},{128,96},{160,128},{192,160},{224,192},{256... | collective-permute-start | bytes 786440 | tf_op jit(solution)/shard_map/ppermute | solution.py:365
  10.2 2.1 %collective-permute-start = (bf16[64,4096]{1,0:T(8,128)(2,1)S(1)}, bf16[64,4096]{1,0:T(8,128)(2,1)}, u32[]{:S(2)}, u32[]{:S(2)}) collective-permute-start(bf16[64,4096]{1,0:T(8,128)(2,1)S(1)} %get-tuple-element.17), channel_id=1, source_target_pairs={{0,32},{32,64},{64,96},{96,128},{128,160},{160,192},{192,224},{224... | collective-permute-start | bytes 1572872 | tf_op jit(solution)/shard_map/ppermute | solution.py:364
  12.3 0.4 multiply_reduce_fusion
  12.7 0.5 fusion.10
  13.3 0.7 iota_multiply_fusion.1
  14.0 0.3 divide_multiply_fusion.w_ref
  14.3 1.1 sine_multiply_fusion
  15.5 3.5 %subtract_convert_fusion = bf16[2,32,32,1024]{3,2,1,0:T(8,128)(2,1)} fusion(f32[2,32,1024]{2,1,0:T(8,128)S(1)} %get-tuple-element.22, f32[32,1024]{1,0:T(8,128)S(1)} %get-tuple-element.21, f32[2,32,1024]{2,1,0:T(8,128)S(1)} %get-tuple-element.20, f32[32,1024]{1,0:T(8,128)S(1)} %get-tuple-element.19), kind=kLoop, calls=%fused_computation | loop fusion | flops 8388608 | bytes 4980736 | tf_op jit(solution)/shard_map/convert_element_type | solution.py:55
  19.1 0.6 prefilter.1.p_ref
  19.6 0.2 cosine_multiply_fusion.2
  19.8 4.2 %collective-permute-done.back_ref = bf16[64,4096]{1,0:T(8,128)(2,1)} collective-permute-done((bf16[64,4096]{1,0:T(8,128)(2,1)S(1)}, bf16[64,4096]{1,0:T(8,128)(2,1)}, u32[]{:S(2)}, u32[]{:S(2)}) %collective-permute-start) | collective-permute-done | bytes 524320 | tf_op jit(solution)/shard_map/ppermute | solution.py:364
  24.0 5.6 %channelize.1 = bf16[256,2,8,128]{3,2,1,0:T(8,128)(2,1)} custom-call(f32[4,64,2048]{2,1,0:T(8,128)S(1)} %prefilter.1.p_ref, bf16[64,4096]{1,0:T(8,128)(2,1)} %collective-permute-done.back_ref, bf16[64,2048]{1,0:T(8,128)(2,1)} %collective-permute-done.1.ahead_ref, f32[4,2048]{1,0:T(4,128)S(1)} %divide_multiply_fusion.w_ref, bf16[2048,1024]{1,0:T(8,128)(2,1)} %bitcast.29), custom_call_target="tpu_custom_call" | custom-call | tf_op jit(solution)/shard_map/channelize/pallas_call | solution.py:175
  29.6 22.8 %all-to-all-start = ((bf16[512,8,128]{2,1,0:T(8,128)(2,1)}), bf16[512,8,128]{2,1,0:T(8,128)(2,1)S(1)}, u32[]{:S(2)}, u32[]{:S(2)}) async-start(bf16[512,8,128]{2,1,0:T(8,128)(2,1)} %bitcast.2), calls=%async_computation | async-start | bytes 2097152 | tf_op jit(solution)/shard_map/all_to_all | solution.py:369
  52.6 0.1 mul.589
  52.9 0.3 sine_multiply_fusion.1
  53.2 0.1 reshape.397
  53.4 5.5 %selection.1.select_ref = bf16[8,2048,256]{2,1,0:T(8,128)(2,1)} custom-call(s32[8,256]{1,0:T(8,128)S(1)} %bitcast.28), custom_call_target="tpu_custom_call" | custom-call | tf_op jit(solution)/shard_map/selection/pallas_call | solution.py:202
  59.0 9.2 %phases.1.t_ref = bf16[2,1024,1024]{2,1,0:T(8,128)(2,1)} custom-call(s32[2]{0:T(128)S(1)} %pad_add_fusion.1.num_ref, s32[1024,512]{1,0:T(8,128)S(1)} %copy-done.2, f32[8,128]{1,0:T(8,128)S(1)} %maximum_maximum_fusion.lut_ref), custom_call_target="tpu_custom_call" | custom-call | tf_op jit(solution)/shard_map/phases/pallas_call | solution.py:322
  68.4 0.1 pad_maximum_fusion.1
  68.4 0.2 subtract_convert_fusion.1
  68.7 16.0 %all-to-all-done = bf16[512,8,128]{2,1,0:T(8,128)(2,1)S(1)} async-done(((bf16[512,8,128]{2,1,0:T(8,128)(2,1)}), bf16[512,8,128]{2,1,0:T(8,128)(2,1)S(1)}, u32[]{:S(2)}, u32[]{:S(2)}) %all-to-all-start) | async-done | bytes 1048608 | tf_op jit(solution)/shard_map/all_to_all | solution.py:369
  84.7 11.4 %beams.1 = bf16[1024,128]{1,0:T(8,128)(2,1)S(1)} custom-call(bf16[2,4,16,4,8,128]{5,4,3,2,1,0:T(8,128)(2,1)S(1)} %bitcast.24, bf16[8,2048,256]{2,1,0:T(8,128)(2,1)} %selection.1.select_ref, bf16[2,256,512]{2,1,0:T(8,128)(2,1)S(1)} %pad_maximum_fusion.ns_ref, f32[2,32]{1,0:T(2,128)S(1)} %maximum_convert_fusion.1.ew_ref, bf16[64,64]{1,0:T(8,128)(2,1)S(1)} %bitcast.27), custom_call_target="tpu_custom_call" | custom-call | tf_op jit(solution)/shard_map/beams/pallas_call | solution.py:280
  96.0 26.8 %all_to_all.15 = bf16[512,2,128]{2,1,0:T(2,128)(2,1)S(1)} all-to-all(bf16[512,2,128]{2,1,0:T(2,128)(2,1)S(1)} %bitcast.26), channel_id=1, replica_groups=mesh['y'=8,'z_lo'=2,'z_hi'=4,'x'=4,'core'=2] {'core','z_hi','z_lo','y','x'}, dimensions={0} | all-to-all | bytes 524288 | tf_op jit(solution)/shard_map/all_to_all | solution.py:386
  122.8 1.6 %search.1 = bf16[512,128]{1,0:T(8,128)(2,1)} custom-call(bf16[1024,128]{1,0:T(8,128)(2,1)S(1)} %bitcast.25, bf16[2,1024,1024]{2,1,0:T(8,128)(2,1)S(1)} %copy-done), custom_call_target="tpu_custom_call" | custom-call | tf_op jit(solution)/shard_map/search/pallas_call | solution.py:348
  124.4 3.5 %all-to-all-start.2 = ((bf16[16,32,128]{2,1,0:T(8,128)(2,1)}), bf16[16,32,128]{2,1,0:T(8,128)(2,1)S(1)}, u32[]{:S(2)}, u32[]{:S(2)}) async-start(bf16[16,32,128]{2,1,0:T(8,128)(2,1)} %bitcast.12), calls=%async_computation.2 | async-start | bytes 262144 | tf_op jit(solution)/shard_map/all_to_all | solution.py:388
  128.0 0.1 mul.602
  128.1 0.1 copy.9
  128.2 0.1 copy_multiply_fusion
  128.3 8.4 %all-to-all-done.2 = bf16[16,32,128]{2,1,0:T(8,128)(2,1)S(1)} async-done(((bf16[16,32,128]{2,1,0:T(8,128)(2,1)}), bf16[16,32,128]{2,1,0:T(8,128)(2,1)S(1)}, u32[]{:S(2)}, u32[]{:S(2)}) %all-to-all-start.2) | async-done | bytes 131104 | tf_op jit(solution)/shard_map/all_to_all | solution.py:388
  136.7 0.2 reshape.402
  136.9 1.3 convolution_bitcast_fusion
  (37 shorter events, 0.9 us)
Async XLA Ops:
  0.0 19.1 %copy-start.1 = (s32[64,8192]{1,0:T(8,128)S(1)}, s32[64,8192]{1,0:T(8,128)}, u32[]{:S(2)}) copy-start(s32[64,8192]{1,0:T(8,128)} %v_ref.3) | copy-start | bytes 6291460
  2.5 17.3 %collective-permute-start.1 = (bf16[64,2048]{1,0:T(8,128)(2,1)S(1)}, bf16[64,2048]{1,0:T(8,128)(2,1)}, u32[]{:S(2)}, u32[]{:S(2)}) collective-permute-start(bf16[64,2048]{1,0:T(8,128)(2,1)S(1)} %get-tuple-element.18), channel_id=1, source_target_pairs={{32,0},{64,32},{96,64},{128,96},{160,128},{192,160},{224,192},{256... | collective-permute-start | bytes 786440 | tf_op jit(solution)/shard_map/ppermute | solution.py:365
  10.2 13.8 %collective-permute-start = (bf16[64,4096]{1,0:T(8,128)(2,1)S(1)}, bf16[64,4096]{1,0:T(8,128)(2,1)}, u32[]{:S(2)}, u32[]{:S(2)}) collective-permute-start(bf16[64,4096]{1,0:T(8,128)(2,1)S(1)} %get-tuple-element.17), channel_id=1, source_target_pairs={{0,32},{32,64},{64,96},{96,128},{128,160},{160,192},{192,224},{224... | collective-permute-start | bytes 1572872 | tf_op jit(solution)/shard_map/ppermute | solution.py:364
  19.0 33.8 %copy-start.4 = (s32[256]{0:T(256)S(1)}, s32[256]{0:T(256)}, u32[]{:S(2)}) copy-start(s32[256]{0:T(256)} %param.8) | copy-start | bytes 3076
  19.0 34.2 %copy-start.3 = (s32[2048]{0:T(1024)S(1)}, s32[2048]{0:T(1024)}, u32[]{:S(2)}) copy-start(s32[2048]{0:T(1024)} %param.6) | copy-start | bytes 24580
  24.0 35.0 %copy-start.2 = (s32[1024,512]{1,0:T(8,128)S(1)}, s32[1024,512]{1,0:T(8,128)}, u32[]{:S(2)}) copy-start(s32[1024,512]{1,0:T(8,128)} %d_ref.1) | copy-start | bytes 6291460
  29.6 55.1 %all-to-all-start = ((bf16[512,8,128]{2,1,0:T(8,128)(2,1)}), bf16[512,8,128]{2,1,0:T(8,128)(2,1)S(1)}, u32[]{:S(2)}, u32[]{:S(2)}) async-start(bf16[512,8,128]{2,1,0:T(8,128)(2,1)} %bitcast.2), calls=%async_computation | async-start | bytes 2097152 | tf_op jit(solution)/shard_map/all_to_all | solution.py:369
  84.7 38.1 %copy-start = (bf16[2,1024,1024]{2,1,0:T(8,128)(2,1)S(1)}, bf16[2,1024,1024]{2,1,0:T(8,128)(2,1)}, u32[]{:S(2)}) copy-start(bf16[2,1024,1024]{2,1,0:T(8,128)(2,1)} %phases.1.t_ref) | copy-start | bytes 12582916
  124.4 12.2 %all-to-all-start.2 = ((bf16[16,32,128]{2,1,0:T(8,128)(2,1)}), bf16[16,32,128]{2,1,0:T(8,128)(2,1)S(1)}, u32[]{:S(2)}, u32[]{:S(2)}) async-start(bf16[16,32,128]{2,1,0:T(8,128)(2,1)} %bitcast.12), calls=%async_computation.2 | async-start | bytes 262144 | tf_op jit(solution)/shard_map/all_to_all | solution.py:388

commit v4 on v3

--- a/solution.py
+++ b/solution.py
@@ -244,7 +244,7 @@
         quarter = iota((16, 128), 1) // 32
         for c in range(2):
 
-            def east(e, _):
+            def east_beam(e):
                 power = None
                 for pol in range(2):
                     real = 0.5 * y_ref[c, 0, pol, 0]
@@ -270,9 +270,13 @@
                         bh = half * 4 + low
                         start = ((bh % 2) * 256 + e * 64 + bh // 2) * 2 + c
                         s_ref[pl.ds(start, 16, stride=8), :] = rows
+
+            def east(i, _):
+                east_beam(2 * i)
+                east_beam(2 * i + 1)
                 return 0
 
-            lax.fori_loop(0, 4, east, 0)
+            lax.fori_loop(0, 2, east, 0)
         o_ref[...] = s_ref[...].astype(BF16)
 
 
@@ -298,13 +302,13 @@
     first_k = num_ref[0]
     plain = num_ref[1].astype(F32)
     scale = 1.0 - plain
-    cos_lut = jnp.broadcast_to(lut_ref[0:1, :], (64, 128))
-    sin_lut = jnp.broadcast_to(lut_ref[1:2, :], (64, 128))
+    cos_lut = jnp.broadcast_to(lut_ref[0:1, :], (256, 128))
+    sin_lut = jnp.broadcast_to(lut_ref[1:2, :], (256, 128))
     for parity in range(2):
 
         def fill(i, _):
-            at = pl.ds(pl.multiple_of(parity * 512 + i * 64, 64), 64)
-            delays = d_ref[pl.ds(i * 128 + parity, 64, stride=2), :]
+            at = pl.ds(pl.multiple_of(parity * 512 + i * 256, 256), 256)
+            delays = d_ref[pl.ds(i * 512 + parity, 256, stride=2), :]
             turn = (first_k * delays) & (SPECTRA - 1)
             cos = jnp.take_along_axis(cos_lut, turn, axis=1)
             sin = jnp.take_along_axis(sin_lut, turn, axis=1)
@@ -315,7 +319,7 @@
             o_ref[1, at, 128:] = (-scale * sign * sin).astype(BF16)
             return 0
 
-        lax.fori_loop(0, 8, fill, 0)
+        lax.fori_loop(0, 2, fill, 0)
 
 
 def phase_tables(numbers, delays, lut):
@@ -366,28 +370,28 @@
     window = pfb_window() * (1.0 / 64.0)
     keep = jnp.where(tm == 15, 0, 1).astype(jnp.int32).reshape(1)
     spectra = channelize(prefilter(keep, voltages, window), back, ahead, window, twiddle_tables())
-    received = lax.all_to_all(spectra, everyone, split_axis=0, concat_axis=0, tiled=True)
-
     chan_ids = (me % 256) * 4 + me // 256 + 2 * jnp.arange(2, dtype=jnp.int32) + CHANS
     ew = steer_seed(jnp.arange(4, dtype=jnp.int32), ew_grid, chan_ids, 0.5)
     ew = jnp.stack([x.astype(BF16).astype(F32).transpose(0, 2, 1).reshape(32) for x in ew])
-    slots = feed_at_grid_slot.reshape(ROWS, 8).T
     forward, backward = time_rows()
+    backward = backward.reshape(4, 2, 8, SPECTRA).transpose(0, 2, 1, 3).reshape(4, 16, SPECTRA)
     angles = jnp.arange(128, dtype=jnp.int32) % SPECTRA
     angles = angles.astype(F32) * (TWO_PI / SPECTRA)
     lut = jnp.stack([jnp.cos(angles), jnp.sin(angles)] + [jnp.zeros_like(angles)] * 6)
     numbers = jnp.stack([block + 1, jnp.where(block == 15, 1, 0)]).astype(jnp.int32)
+    ns = north_tables(ns_grid, chan_ids)
+    select = selection(feed_at_grid_slot.reshape(ROWS, 8).T)
+    spectra, select, ns, ew, forward, backward, lut, numbers = lax.optimization_barrier(
+        (spectra, select, ns, ew, forward, backward, lut, numbers)
+    )
+    received = lax.all_to_all(spectra, everyone, split_axis=0, concat_axis=0, tiled=True)
+    freq = form_beams(received.reshape(2, 4, 16, 4, 8, 128), in_hbm(select), ns, ew, forward)
+    freq, delays = lax.optimization_barrier((freq, delays))
     tables = phase_tables(numbers, delays, lut)
-    received, tables = lax.optimization_barrier((received, tables))
-    select = pltpu.with_memory_space_constraint(selection(slots), pltpu.HBM)
-    freq = form_beams(
-        received.reshape(2, 4, 16, 4, 8, 128), select, north_tables(ns_grid, chan_ids), ew, forward
-    )
     by_freq = lax.all_to_all(freq.reshape(512, 2, 128), everyone, split_axis=0, concat_axis=0, tiled=True)
     moved = search(by_freq.reshape(CHANS, 128), tables)
     combined = lax.all_to_all(moved.reshape(16, 32, 128), TIME, split_axis=0, concat_axis=0, tiled=True)
     combined = combined.reshape(16, 32, 4, 32)
-    backward = backward.reshape(4, 2, 8, SPECTRA).transpose(0, 2, 1, 3).reshape(4, 16, SPECTRA)
     return jnp.einsum("gdqb,qgt->dbt", combined, backward, preferred_element_type=F32)
 
 

time: 139 us -> 141 us (1.014)
  blocking collectives: 26.8 us -> 62.4 us
  waiting for transfers between devices: 28.6 us -> 11.2 us
  starting transfers between devices: 36.1 us -> 19.1 us
  Pallas kernels: 36.3 us -> 30.9 us
  local copies, waits for them, and re-layouts: 0.94 us -> 4.69 us
  other arithmetic: 7.97 us -> 10.4 us
    all_to_all x1 -> x2, blocking collectives: 26.8 us -> 62.4 us  [the longest x1 51.2 us: local(): lax.all_to_all(spectra, everyone, split_axis=0, concat_axis=0, tiled=True)]
    all_to_all x2 -> x1, starting transfers between devices: 26.3 us -> 9.29 us  [local(): lax.all_to_all(freq.reshape(512, 2, 128), everyone, split_axis=0, concat_...]
    all_to_all x2 -> x1, waiting for transfers between devices: 24.4 us -> 11.2 us  [local(): lax.all_to_all(freq.reshape(512, 2, 128), everyone, split_axis=0, concat_...]
    ppermute x1, waiting for transfers between devices: 4.19 us -> 0.01 us  [local(): back = lax.ppermute(back, TIME, [(i, i + 1) for i in range(15)])]
    pallas_call x1, Pallas kernels: 9.22 us -> 5.87 us  [phase_tables(): pl.pallas_call(phase_kernel, grid=(4,), in_specs=[SMEM, pl.BlockSpec((CHA...]
    unnamed x10 -> x8, local copies, waits for them, and re-layouts: 0.02 us -> 2.2 us
    reshape x2, local copies, waits for them, and re-layouts: 0.15 us -> 1.71 us  [local(): select = selection(feed_at_grid_slot.reshape(ROWS, 8).T)]
  transfers between devices with their start and end apart: 4 -> 3, of which waited for: 3 -> 1; matrix products, arithmetic and copies ran while one was open for 6% -> 9% of each run, Pallas kernels for 11% -> 9%
where the time goes in v4:
time: 141 us; the launch traced here: 140 us
  blocking collectives  62.4 us (44%)
  Pallas kernels  30.9 us (22%)
  starting transfers between devices  19.1 us (14%)
  waiting for transfers between devices  11.2 us (8%)
  other arithmetic  10.4 us (7%)
  local copies, waits for them, and re-layouts  4.69 us (3%)
    all_to_all x1, blocking collectives, local(): lax.all_to_all(spectra, everyone, split_axis=0, concat_axis=0, tiled=True)  51.2 us
    all_to_all x1, blocking collectives, local(): lax.all_to_all(moved.reshape(16, 32, 128), TIME, split_axis=0, concat_axi...  11.2 us
    all_to_all x1, waiting for transfers between devices, local(): lax.all_to_all(freq.reshape(512, 2, 128), everyone, split_axis=0, concat_...  11.2 us
    pallas_call x1, Pallas kernels, form_beams(): pl.pallas_call(beam_kernel, grid=(4,), in_specs=[VMEM, pl.BlockSpec((2, 2...  11.1 us
    all_to_all x1, starting transfers between devices, local(): lax.all_to_all(freq.reshape(512, 2, 128), everyone, split_axis=0, concat_...  9.29 us
    ppermute x1, starting transfers between devices, local(): ahead = lax.ppermute(ahead, TIME, [((i + 1) % 16, i) for i in range(16)])  7.72 us
    pallas_call x1, Pallas kernels, phase_tables(): pl.pallas_call(phase_kernel, grid=(4,), in_specs=[SMEM, pl.BlockSpec((CHA...  5.87 us
    pallas_call x1, Pallas kernels, selection(): pl.pallas_call(select_kernel, grid=(8,), in_specs=[VMEM], out_specs=pl.Bl...  5.48 us
  transfers between devices with their start and end apart: 3, of which 1 were waited for; matrix products, arithmetic and copies ran while one was open for 9% of the time, Pallas kernels for 9%

profile of v4, /device:TPU:1, one launch (start us, length us, event | category | flops | bytes accessed | tf_op | source)
XLA Modules:
  0.0 140.2 jit_solution(206302085237315144)
XLA Ops:
  0.0 2.3 %edges.1 = (bf16[64,4096]{1,0:T(8,128)(2,1)S(1)}, bf16[64,2048]{1,0:T(8,128)(2,1)S(1)}) custom-call(s32[64,8192]{1,0:T(8,128)} %v_ref.3), custom_call_target="tpu_custom_call" | custom-call | tf_op jit(solution)/shard_map/edges/pallas_call | solution.py:119
  2.3 7.7 %collective-permute-start.1 = (bf16[64,2048]{1,0:T(8,128)(2,1)S(1)}, bf16[64,2048]{1,0:T(8,128)(2,1)}, u32[]{:S(2)}, u32[]{:S(2)}) collective-permute-start(bf16[64,2048]{1,0:T(8,128)(2,1)S(1)} %get-tuple-element.26), channel_id=1, source_target_pairs={{32,0},{64,32},{96,64},{128,96},{160,128},{192,160},{224,192},{256... | collective-permute-start | bytes 786440 | tf_op jit(solution)/shard_map/ppermute | solution.py:369
  10.1 2.1 %collective-permute-start = (bf16[64,4096]{1,0:T(8,128)(2,1)S(1)}, bf16[64,4096]{1,0:T(8,128)(2,1)}, u32[]{:S(2)}, u32[]{:S(2)}) collective-permute-start(bf16[64,4096]{1,0:T(8,128)(2,1)S(1)} %get-tuple-element.25), channel_id=1, source_target_pairs={{0,32},{32,64},{64,96},{96,128},{128,160},{160,192},{192,224},{224... | collective-permute-start | bytes 1572872 | tf_op jit(solution)/shard_map/ppermute | solution.py:368
  12.3 0.4 multiply_reduce_fusion
  12.7 1.2 fusion.10
  14.1 0.7 iota_multiply_fusion.1
  14.9 0.1 mul.586
  15.1 0.2 cosine_multiply_fusion.2
  15.4 0.3 divide_multiply_fusion.w_ref
  15.7 0.8 iota_multiply_fusion
  16.5 0.3 sine_multiply_fusion.1
  16.8 1.1 sine_multiply_fusion
  18.0 0.2 subtract_convert_fusion.1
  18.3 4.5 %subtract_convert_fusion = bf16[2,32,32,1024]{3,2,1,0:T(8,128)(2,1)} fusion(f32[2,32,1024]{2,1,0:T(8,128)S(1)} %get-tuple-element.30, f32[32,1024]{1,0:T(8,128)} %get-tuple-element.29, f32[2,32,1024]{2,1,0:T(8,128)S(1)} %get-tuple-element.28, f32[32,1024]{1,0:T(8,128)} %get-tuple-element.27), kind=kLoop, calls=%fused_computation | loop fusion | flops 8388608 | bytes 4980736 | tf_op jit(solution)/shard_map/convert_element_type | solution.py:55
  22.9 0.1 mul.599
  23.0 0.1 copy.9
  23.1 0.8 reshape.396
  23.8 1.0 copy.8
  24.8 5.5 %selection.1.select_ref = bf16[8,2048,256]{2,1,0:T(8,128)(2,1)} custom-call(s32[8,256]{1,0:T(8,128)S(1)} %bitcast.29), custom_call_target="tpu_custom_call" | custom-call | tf_op jit(solution)/shard_map/selection/pallas_call | solution.py:202
  30.3 0.6 prefilter.1.p_ref
  30.9 0.1 copy_multiply_fusion
  31.0 4.6 %channelize.1 = bf16[256,2,8,128]{3,2,1,0:T(8,128)(2,1)S(1)} custom-call(f32[4,64,2048]{2,1,0:T(8,128)S(1)} %prefilter.1.p_ref, bf16[64,4096]{1,0:T(8,128)(2,1)} %collective-permute-done.back_ref, bf16[64,2048]{1,0:T(8,128)(2,1)} %collective-permute-done.1.ahead_ref, f32[4,2048]{1,0:T(4,128)S(1)} %divide_multiply_fusion.w_ref, bf16[2048,1024]{1,0:T(8,128)(2,1)} %bitcast.30), custom_call_target="tpu_custom_call" | custom-call | tf_op jit(solution)/shard_map/channelize/pallas_call | solution.py:175
  35.6 51.2 %all_to_all.15 = bf16[512,8,128]{2,1,0:T(8,128)(2,1)S(1)} all-to-all(bf16[512,8,128]{2,1,0:T(8,128)(2,1)S(1)} %bitcast.24), channel_id=1, replica_groups=mesh['y'=8,'z_lo'=2,'z_hi'=4,'x'=4,'core'=2] {'core','z_hi','z_lo','y','x'}, dimensions={0} | all-to-all | bytes 2097152 | tf_op jit(solution)/shard_map/all_to_all | solution.py:387
  86.8 11.1 %beams.1 = bf16[1024,128]{1,0:T(8,128)(2,1)} custom-call(bf16[2,4,16,4,8,128]{5,4,3,2,1,0:T(8,128)(2,1)S(1)} %bitcast.25, bf16[8,2048,256]{2,1,0:T(8,128)(2,1)} %selection.1.select_ref, bf16[2,256,512]{2,1,0:T(8,128)(2,1)S(1)} %pad_maximum_fusion.ns_ref, f32[2,32]{1,0:T(2,128)S(1)} %maximum_convert_fusion.1.ew_ref, bf16[64,64]{1,0:T(8,128)(2,1)S(1)} %bitcast.28), custom_call_target="tpu_custom_call" | custom-call | tf_op jit(solution)/shard_map/beams/pallas_call | solution.py:284
  97.9 9.3 %all-to-all-start.1 = ((bf16[512,2,128]{2,1,0:T(2,128)(2,1)}), bf16[512,2,128]{2,1,0:T(2,128)(2,1)S(1)}, u32[]{:S(2)}, u32[]{:S(2)}) async-start(bf16[512,2,128]{2,1,0:T(2,128)(2,1)} %bitcast.13), calls=%async_computation.1 | async-start | bytes 524288 | tf_op jit(solution)/shard_map/all_to_all | solution.py:391
  107.2 5.9 %phases.1.t_ref = bf16[2,1024,1024]{2,1,0:T(8,128)(2,1)} custom-call(s32[2]{0:T(128)S(1)} %pad_add_fusion.1.num_ref, s32[1024,512]{1,0:T(8,128)S(1)} %copy-done.2, f32[8,128]{1,0:T(8,128)S(1)} %maximum_maximum_fusion.lut_ref), custom_call_target="tpu_custom_call" | custom-call | tf_op jit(solution)/shard_map/phases/pallas_call | solution.py:326
  113.1 11.2 %all-to-all-done.1 = bf16[512,2,128]{2,1,0:T(2,128)(2,1)S(1)} async-done(((bf16[512,2,128]{2,1,0:T(2,128)(2,1)}), bf16[512,2,128]{2,1,0:T(2,128)(2,1)S(1)}, u32[]{:S(2)}, u32[]{:S(2)}) %all-to-all-start.1) | async-done | bytes 262176 | tf_op jit(solution)/shard_map/all_to_all | solution.py:391
  124.3 2.2 %copy-done = bf16[2,1024,1024]{2,1,0:T(8,128)(2,1)S(1)} copy-done((bf16[2,1024,1024]{2,1,0:T(8,128)(2,1)S(1)}, bf16[2,1024,1024]{2,1,0:T(8,128)(2,1)}, u32[]{:S(2)}) %copy-start) | copy-done | bytes 4194328
  126.5 1.0 search.1
  127.5 11.2 %all_to_all.16 = bf16[16,32,128]{2,1,0:T(8,128)(2,1)S(1)} all-to-all(bf16[16,32,128]{2,1,0:T(8,128)(2,1)S(1)} %bitcast.27), channel_id=1, replica_groups=mesh['y'=8,'z_lo'=2,'z_hi'=4,'x'=4,'core'=2] {'y','z_lo'}, dimensions={0} | all-to-all | bytes 262144 | tf_op jit(solution)/shard_map/all_to_all | solution.py:393
  138.7 0.2 reshape.403
  138.9 1.3 convolution_bitcast_fusion
  (34 shorter events, 0.8 us)
Async XLA Ops:
  0.0 23.1 %copy-start.3 = (s32[2048]{0:T(1024)S(1)}, s32[2048]{0:T(1024)}, u32[]{:S(2)}) copy-start(s32[2048]{0:T(1024)} %param.6) | copy-start | bytes 24580
  2.3 28.6 %collective-permute-start.1 = (bf16[64,2048]{1,0:T(8,128)(2,1)S(1)}, bf16[64,2048]{1,0:T(8,128)(2,1)}, u32[]{:S(2)}, u32[]{:S(2)}) collective-permute-start(bf16[64,2048]{1,0:T(8,128)(2,1)S(1)} %get-tuple-element.26), channel_id=1, source_target_pairs={{32,0},{64,32},{96,64},{128,96},{160,128},{192,160},{224,192},{256... | collective-permute-start | bytes 786440 | tf_op jit(solution)/shard_map/ppermute | solution.py:369
  10.1 20.9 %collective-permute-start = (bf16[64,4096]{1,0:T(8,128)(2,1)S(1)}, bf16[64,4096]{1,0:T(8,128)(2,1)}, u32[]{:S(2)}, u32[]{:S(2)}) collective-permute-start(bf16[64,4096]{1,0:T(8,128)(2,1)S(1)} %get-tuple-element.25), channel_id=1, source_target_pairs={{0,32},{32,64},{64,96},{96,128},{128,160},{160,192},{192,224},{224... | collective-permute-start | bytes 1572872 | tf_op jit(solution)/shard_map/ppermute | solution.py:368
  12.2 18.1 %copy-start.1 = (s32[64,8192]{1,0:T(8,128)S(1)}, s32[64,8192]{1,0:T(8,128)}, u32[]{:S(2)}) copy-start(s32[64,8192]{1,0:T(8,128)} %v_ref.3) | copy-start | bytes 6291460
  35.6 71.6 %copy-start.2 = (s32[1024,512]{1,0:T(8,128)S(1)}, s32[1024,512]{1,0:T(8,128)}, u32[]{:S(2)}) copy-start(s32[1024,512]{1,0:T(8,128)} %d_ref) | copy-start | bytes 6291460
  97.9 26.4 %all-to-all-start.1 = ((bf16[512,2,128]{2,1,0:T(2,128)(2,1)}), bf16[512,2,128]{2,1,0:T(2,128)(2,1)S(1)}, u32[]{:S(2)}, u32[]{:S(2)}) async-start(bf16[512,2,128]{2,1,0:T(2,128)(2,1)} %bitcast.13), calls=%async_computation.1 | async-start | bytes 524288 | tf_op jit(solution)/shard_map/all_to_all | solution.py:391
  124.3 2.2 %copy-start = (bf16[2,1024,1024]{2,1,0:T(8,128)(2,1)S(1)}, bf16[2,1024,1024]{2,1,0:T(8,128)(2,1)}, u32[]{:S(2)}) copy-start(bf16[2,1024,1024]{2,1,0:T(8,128)(2,1)} %phases.1.t_ref) | copy-start | bytes 12582916

commit v5 on v4

--- a/solution.py
+++ b/solution.py
@@ -81,108 +81,81 @@
     table = jnp.stack([jnp.cos(angles) * factor, -jnp.sin(angles) * factor], axis=1)
     weight = jnp.where(ks == 32, 1.0, 2.0)[:, None, :, None]
     table = table.astype(BF16)
-    return jnp.roll(table, -1, axis=-1).reshape(64, SPECTRA), (table * weight.astype(BF16)).reshape(4, 16, SPECTRA)
-
-
-def prefilter_kernel(keep_ref, v_ref, w_ref, o_ref):
-    for s in range(1, 5):
+    return table.reshape(64, SPECTRA), (table * weight.astype(BF16)).reshape(4, 16, SPECTRA)
+
+
+def in_hbm(x):
+    return pltpu.with_memory_space_constraint(x, pltpu.HBM)
+
+
+def prefilter_kernel(v_ref, w_ref, o_ref):
+    for s in range(4):
         total = None
-        for at in range(max(0, s - 3), min(4, s + 1)):
+        for at in range(s + 1):
             frame = v_ref[:, at * NFFT : (at + 1) * NFFT].astype(F32)
             tap = at - s + 3
             term = w_ref[tap : tap + 1, :] * frame
             total = term if total is None else total + term
-        o_ref[s - 1] = total if s < 4 else jnp.where(keep_ref[0] == 1, total, 0.0)
-
-
-def in_hbm(x):
-    return pltpu.with_memory_space_constraint(x, pltpu.HBM)
-
-
-def whole(shape):
-    return pl.BlockSpec(shape, lambda i: (0, 0))
-
-
-def edges_kernel(v_ref, back_ref, ahead_ref):
-    frame = v_ref[...].astype(BF16)
-
-    @pl.when(pl.program_id(0) < 2)
-    def _():
-        back_ref[...] = frame
-
-    @pl.when(pl.program_id(0) == 2)
-    def _():
-        ahead_ref[...] = frame
-
-
-def edges(voltages):
-    return pl.pallas_call(
-        edges_kernel,
-        grid=(3,),
-        in_specs=[pl.BlockSpec((64, NFFT), lambda i: (0, (i + 2) % 4))],
-        out_specs=[pl.BlockSpec((64, NFFT), lambda i: (0, jnp.minimum(i, 1))), whole((64, NFFT))],
-        out_shape=[jax.ShapeDtypeStruct((64, 2 * NFFT), BF16), jax.ShapeDtypeStruct((64, NFFT), BF16)],
-        compiler_params=LEAN,
-        name="edges",
-    )(voltages)
-
-
-def prefilter(keep, voltages, window):
+        o_ref[s] = total
+
+
+def prefilter(voltages, window):
     return pl.pallas_call(
         prefilter_kernel,
-        in_specs=[SMEM, VMEM, VMEM],
+        in_specs=[VMEM, VMEM],
         out_specs=VMEM,
         out_shape=jax.ShapeDtypeStruct((4, 64, NFFT), F32),
         compiler_params=LEAN,
         name="prefilter",
-    )(keep, voltages, window)
-
-
-def channelize_kernel(p_ref, back_ref, ahead_ref, w_ref, t_ref, o_ref, x_ref):
-    @pl.when(pl.program_id(0) == 0)
-    def _():
-        def filter_rows(i, _):
-            at = pl.ds(pl.multiple_of(i * 16, 16), 16)
-
-            def term(tap, ref, frame):
-                return w_ref[tap : tap + 1, :] * ref[at, frame * NFFT : (frame + 1) * NFFT].astype(F32)
-
-            for s in range(4):
-                total = p_ref[s, at, :]
-                if s == 0:
-                    total = total + term(0, back_ref, 0) + term(1, back_ref, 1)
-                elif s == 1:
-                    total = total + term(0, back_ref, 1)
-                elif s == 3:
-                    total = total + term(3, ahead_ref, 0)
-                low, high = total[:, :HALF], total[:, HALF:]
+    )(voltages, window)
+
+
+def channelize_kernel(p_ref, h_ref, w_ref, t_ref, o_ref, x_ref):
+    def filter_rows(i, _):
+        at = pl.ds(pl.multiple_of(i * 16, 16), 16)
+        for s in range(4):
+            for half in range(2):
+                parts = []
+                for sign in range(2):
+                    first = sign * HALF + half * 512
+                    total = p_ref[s, at, first : first + 512]
+                    for frame in range(s, 3):
+                        tap = frame - s
+                        lanes = frame * NFFT + first
+                        total = total + w_ref[tap : tap + 1, first : first + 512] * h_ref[
+                            at, lanes : lanes + 512
+                        ].astype(F32)
+                    parts.append(total)
                 to = pl.ds(pl.multiple_of(s * 64 + i * 16, 16), 16)
-                x_ref[0, to, :] = (low + high).astype(BF16)
-                x_ref[1, to, :] = (low - high).astype(BF16)
-            return 0
-
-        lax.fori_loop(0, 4, filter_rows, 0)
-
+                x_ref[0, to, half * 512 : half * 512 + 512] = (parts[0] + parts[1]).astype(BF16)
+                x_ref[1, to, half * 512 : half * 512 + 512] = (parts[0] - parts[1]).astype(BF16)
+        return 0
+
+    lax.fori_loop(0, 4, filter_rows, 0)
     upper = iota((64, 8, 128), 1) < 4
-    acc = lax.dot_general(t_ref[...], x_ref[pl.program_id(0) // 2], NT, preferred_element_type=F32)
-    first = acc[:, :128].reshape(64, 8, 128)
-    second = acc[:, 128:].reshape(64, 8, 128)
-    o_ref[:, 0] = jnp.where(upper, first, pltpu.roll(second, 4, 1)).astype(BF16)
-    o_ref[:, 1] = jnp.where(upper, pltpu.roll(first, 4, 1), second).astype(BF16)
-
-
-def channelize(partial_sums, back, ahead, window, table):
+
+    def transform(i, _):
+        acc = lax.dot_general(t_ref[i], x_ref[i // 2], NT, preferred_element_type=F32)
+        first = acc[:, :128].reshape(64, 8, 128)
+        second = acc[:, 128:].reshape(64, 8, 128)
+        at = pl.ds(pl.multiple_of(i * 64, 64), 64)
+        o_ref[at, 0] = jnp.where(upper, first, pltpu.roll(second, 4, 1)).astype(BF16)
+        o_ref[at, 1] = jnp.where(upper, pltpu.roll(first, 4, 1), second).astype(BF16)
+        return 0
+
+    lax.fori_loop(0, 4, transform, 0)
+
+
+def channelize(partial_sums, halo, window, table):
     out = pl.pallas_call(
         channelize_kernel,
-        grid=(4,),
-        in_specs=[VMEM, whole((64, 2 * NFFT)), whole((64, NFFT)), VMEM]
-        + [pl.BlockSpec((512, HALF), lambda i: (i, 0))],
-        out_specs=pl.BlockSpec((64, 2, 8, 128), lambda i: (i, 0, 0, 0)),
+        in_specs=[VMEM] * 4,
+        out_specs=VMEM,
         out_shape=jax.ShapeDtypeStruct((256, 2, 8, 128), BF16),
         scratch_shapes=[pltpu.VMEM((2, 256, HALF), BF16)],
         compiler_params=LEAN,
         name="channelize",
-    )(partial_sums, in_hbm(back), in_hbm(ahead), window, in_hbm(table.reshape(2048, HALF)))
+    )(partial_sums, halo, window, table.reshape(4, 512, HALF))
     return out.reshape(512, 8, 128)
 
 
@@ -360,38 +333,35 @@
 
 
 def local(voltages, feed_at_grid_slot, ew_grid, ns_grid, delays):
-    tm = lax.axis_index(TIME)
     everyone = ("core", "z_hi", "z_lo", "y", "x")
     me = lax.axis_index(everyone)
     block = lax.axis_index(("z_lo", "y"))
-    back, ahead = edges(in_hbm(voltages))
-    back = lax.ppermute(back, TIME, [(i, i + 1) for i in range(15)])
-    ahead = lax.ppermute(ahead, TIME, [((i + 1) % 16, i) for i in range(16)])
+    tail = voltages[:, NFFT:].astype(BF16)
+    halo = lax.ppermute(tail, TIME, [(i, i + 1) for i in range(15)])
     window = pfb_window() * (1.0 / 64.0)
-    keep = jnp.where(tm == 15, 0, 1).astype(jnp.int32).reshape(1)
-    spectra = channelize(prefilter(keep, voltages, window), back, ahead, window, twiddle_tables())
+    spectra = channelize(prefilter(voltages, window), halo, window, twiddle_tables())
+    received = lax.all_to_all(spectra, everyone, split_axis=0, concat_axis=0, tiled=True)
+
     chan_ids = (me % 256) * 4 + me // 256 + 2 * jnp.arange(2, dtype=jnp.int32) + CHANS
     ew = steer_seed(jnp.arange(4, dtype=jnp.int32), ew_grid, chan_ids, 0.5)
     ew = jnp.stack([x.astype(BF16).astype(F32).transpose(0, 2, 1).reshape(32) for x in ew])
+    slots = feed_at_grid_slot.reshape(ROWS, 8).T
     forward, backward = time_rows()
-    backward = backward.reshape(4, 2, 8, SPECTRA).transpose(0, 2, 1, 3).reshape(4, 16, SPECTRA)
     angles = jnp.arange(128, dtype=jnp.int32) % SPECTRA
     angles = angles.astype(F32) * (TWO_PI / SPECTRA)
     lut = jnp.stack([jnp.cos(angles), jnp.sin(angles)] + [jnp.zeros_like(angles)] * 6)
     numbers = jnp.stack([block + 1, jnp.where(block == 15, 1, 0)]).astype(jnp.int32)
-    ns = north_tables(ns_grid, chan_ids)
-    select = selection(feed_at_grid_slot.reshape(ROWS, 8).T)
-    spectra, select, ns, ew, forward, backward, lut, numbers = lax.optimization_barrier(
-        (spectra, select, ns, ew, forward, backward, lut, numbers)
+    tables = phase_tables(numbers, delays, lut)
+    received, tables = lax.optimization_barrier((received, tables))
+    select = pltpu.with_memory_space_constraint(selection(slots), pltpu.HBM)
+    freq = form_beams(
+        received.reshape(2, 4, 16, 4, 8, 128), select, north_tables(ns_grid, chan_ids), ew, forward
     )
-    received = lax.all_to_all(spectra, everyone, split_axis=0, concat_axis=0, tiled=True)
-    freq = form_beams(received.reshape(2, 4, 16, 4, 8, 128), in_hbm(select), ns, ew, forward)
-    freq, delays = lax.optimization_barrier((freq, delays))
-    tables = phase_tables(numbers, delays, lut)
     by_freq = lax.all_to_all(freq.reshape(512, 2, 128), everyone, split_axis=0, concat_axis=0, tiled=True)
     moved = search(by_freq.reshape(CHANS, 128), tables)
     combined = lax.all_to_all(moved.reshape(16, 32, 128), TIME, split_axis=0, concat_axis=0, tiled=True)
     combined = combined.reshape(16, 32, 4, 32)
+    backward = backward.reshape(4, 2, 8, SPECTRA).transpose(0, 2, 1, 3).reshape(4, 16, SPECTRA)
     return jnp.einsum("gdqb,qgt->dbt", combined, backward, preferred_element_type=F32)
 
 

time: 141 us -> 136 us (0.965)
  blocking collectives: 62.4 us -> 26.8 us
  waiting for transfers between devices: 11.2 us -> 33.9 us
  starting transfers between devices: 19.1 us -> 35.2 us
  Pallas kernels: 30.9 us -> 27.4 us
  other arithmetic: 10.4 us -> 8.12 us
  local copies, waits for them, and re-layouts: 4.69 us -> 2.45 us
    all_to_all x2 -> x1, blocking collectives: 62.4 us -> 26.8 us  [local(): lax.all_to_all(freq.reshape(512, 2, 128), everyone, split_axis=0, concat_...]
    all_to_all x1 -> x2, starting transfers between devices: 9.29 us -> 30.3 us  [the longest x1 26.8 us: local(): lax.all_to_all(spectra, everyone, split_axis=0, concat_axis=0, tiled=True)]
    all_to_all x1 -> x2, waiting for transfers between devices: 11.2 us -> 28 us  [the longest x1 19.7 us: local(): lax.all_to_all(spectra, everyone, split_axis=0, concat_axis=0, tiled=True)]
    ppermute x2 -> x1, waiting for transfers between devices: 0.01 us -> 5.87 us  [local(): halo = lax.ppermute(tail, TIME, [(i, i + 1) for i in range(15)])]
    ppermute x2 -> x1, starting transfers between devices: 9.85 us -> 4.86 us  [local(): halo = lax.ppermute(tail, TIME, [(i, i + 1) for i in range(15)])]
    pallas_call x3 -> x2, Pallas kernels: 7.47 us -> 3.82 us  [the longest x1 3.37 us: channelize(): pl.pallas_call(channelize_kernel, in_specs=[VMEM] * 4, out_specs=VMEM, ou...]
    convert_element_type x1, other arithmetic: 4.45 us -> 1.51 us  [twiddle_tables(): return table.astype(BF16).reshape(2, 1024, HALF)]
    reshape x2, local copies, waits for them, and re-layouts: 1.71 us -> 0.16 us  [local(): slots = feed_at_grid_slot.reshape(ROWS, 8).T]
  transfers between devices with their start and end apart: 3 -> 3, of which waited for: 1 -> 3; matrix products, arithmetic and copies ran while one was open for 9% -> 5% of each run, Pallas kernels for 9% -> 9%
where the time goes in v5:
time: 136 us; the launch traced here: 135 us
  starting transfers between devices  35.2 us (26%)
  waiting for transfers between devices  33.9 us (25%)
  Pallas kernels  27.4 us (20%)
  blocking collectives  26.8 us (20%)
  other arithmetic  8.12 us (6%)
  local copies, waits for them, and re-layouts  2.45 us (2%)
    all_to_all x1, starting transfers between devices, local(): lax.all_to_all(spectra, everyone, split_axis=0, concat_axis=0, tiled=True)  26.8 us
    all_to_all x1, blocking collectives, local(): lax.all_to_all(freq.reshape(512, 2, 128), everyone, split_axis=0, concat_...  26.8 us
    all_to_all x1, waiting for transfers between devices, local(): lax.all_to_all(spectra, everyone, split_axis=0, concat_axis=0, tiled=True)  19.7 us
    pallas_call x1, Pallas kernels, form_beams(): pl.pallas_call(beam_kernel, grid=(4,), in_specs=[VMEM, pl.BlockSpec((2, 2...  10.6 us
    all_to_all x1, waiting for transfers between devices, local(): lax.all_to_all(moved.reshape(16, 32, 128), TIME, split_axis=0, concat_axi...  8.38 us
    pallas_call x1, Pallas kernels, phase_tables(): pl.pallas_call(phase_kernel, grid=(4,), in_specs=[SMEM, pl.BlockSpec((CHA...  5.88 us
    ppermute x1, waiting for transfers between devices, local(): halo = lax.ppermute(tail, TIME, [(i, i + 1) for i in range(15)])  5.87 us
    pallas_call x1, Pallas kernels, selection(): pl.pallas_call(select_kernel, grid=(8,), in_specs=[VMEM], out_specs=pl.Bl...  5.48 us
  transfers between devices with their start and end apart: 3, of which 3 were waited for; matrix products, arithmetic and copies ran while one was open for 5% of the time, Pallas kernels for 9%

profile of v5, /device:TPU:1, one launch (start us, length us, event | category | flops | bytes accessed | tf_op | source)
XLA Modules:
  0.0 135.3 jit_solution(776442715454773578)
XLA Ops:
  0.0 1.5 %slice_convert_fusion = bf16[64,6144]{1,0:T(8,128)(2,1)S(1)} fusion(s32[64,8192]{1,0:T(8,128)} %v_ref.1), kind=kLoop, calls=%fused_computation.1 | loop fusion | flops 393216 | bytes 2359296 | tf_op jit(solution)/shard_map/convert.1
  1.5 4.9 %collective-permute-start = (bf16[64,6144]{1,0:T(8,128)(2,1)S(1)}, bf16[64,6144]{1,0:T(8,128)(2,1)S(1)}, u32[]{:S(2)}, u32[]{:S(2)}) collective-permute-start(bf16[64,6144]{1,0:T(8,128)(2,1)S(1)} %slice_convert_fusion), channel_id=1, source_target_pairs={{0,32},{32,64},{64,96},{96,128},{128,160},{160,192},{192,224},{224... | collective-permute-start | bytes 2359304 | tf_op jit(solution)/shard_map/ppermute | solution.py:340
  6.4 0.5 fusion.10
  7.0 0.4 multiply_reduce_fusion
  7.4 0.8 iota_multiply_fusion
  8.1 0.3 sine_multiply_fusion.1
  8.5 0.3 divide_multiply_fusion.w_ref
  8.8 1.1 sine_multiply_fusion
  10.0 1.6 %copy-done.1 = s32[64,8192]{1,0:T(8,128)S(1)} copy-done((s32[64,8192]{1,0:T(8,128)S(1)}, s32[64,8192]{1,0:T(8,128)}, u32[]{:S(2)}) %copy-start.1) | copy-done | bytes 2097176
  11.6 0.5 prefilter.1.p_ref
  12.0 0.7 iota_multiply_fusion.1
  12.8 1.5 %subtract_convert_fusion = bf16[2,32,32,1024]{3,2,1,0:T(8,128)(2,1)S(1)} fusion(f32[2,32,1024]{2,1,0:T(8,128)S(1)} %get-tuple-element.18, f32[32,1024]{1,0:T(8,128)S(1)} %get-tuple-element.17, f32[2,32,1024]{2,1,0:T(8,128)S(1)} %get-tuple-element.16, f32[32,1024]{1,0:T(8,128)S(1)} %get-tuple-element.15), kind=kLoop, calls=%fused_computation | loop fusion | flops 8388608 | bytes 4980736 | tf_op jit(solution)/shard_map/convert_element_type | solution.py:55
  14.3 5.9 %collective-permute-done.h_ref = bf16[64,6144]{1,0:T(8,128)(2,1)S(1)} collective-permute-done((bf16[64,6144]{1,0:T(8,128)(2,1)S(1)}, bf16[64,6144]{1,0:T(8,128)(2,1)S(1)}, u32[]{:S(2)}, u32[]{:S(2)}) %collective-permute-start) | collective-permute-done | bytes 786464 | tf_op jit(solution)/shard_map/ppermute | solution.py:340
  20.2 3.4 %channelize.1 = bf16[256,2,8,128]{3,2,1,0:T(8,128)(2,1)} custom-call(f32[4,64,2048]{2,1,0:T(8,128)S(1)} %prefilter.1.p_ref, bf16[64,6144]{1,0:T(8,128)(2,1)S(1)} %collective-permute-done.h_ref, f32[4,2048]{1,0:T(4,128)S(1)} %divide_multiply_fusion.w_ref, bf16[4,512,1024]{2,1,0:T(8,128)(2,1)S(1)} %bitcast.22), custom_call_target="tpu_custom_call" | custom-call | tf_op jit(solution)/shard_map/channelize/pallas_call | solution.py:150
  23.5 26.8 %all-to-all-start = ((bf16[512,8,128]{2,1,0:T(8,128)(2,1)}), bf16[512,8,128]{2,1,0:T(8,128)(2,1)S(1)}, u32[]{:S(2)}, u32[]{:S(2)}) async-start(bf16[512,8,128]{2,1,0:T(8,128)(2,1)} %bitcast.1), calls=%async_computation | async-start | bytes 2097152 | tf_op jit(solution)/shard_map/all_to_all | solution.py:343
  50.4 0.1 mul.585
  50.6 0.1 reshape.393
  50.8 5.5 %selection.1.select_ref = bf16[8,2048,256]{2,1,0:T(8,128)(2,1)} custom-call(s32[8,256]{1,0:T(8,128)S(1)} %bitcast.28), custom_call_target="tpu_custom_call" | custom-call | tf_op jit(solution)/shard_map/selection/pallas_call | solution.py:175
  56.5 5.9 %phases.1.t_ref = bf16[2,1024,1024]{2,1,0:T(8,128)(2,1)} custom-call(s32[2]{0:T(128)S(1)} %pad_add_fusion.1.num_ref, s32[1024,512]{1,0:T(8,128)S(1)} %copy-done.2, f32[8,128]{1,0:T(8,128)S(1)} %maximum_maximum_fusion.lut_ref), custom_call_target="tpu_custom_call" | custom-call | tf_op jit(solution)/shard_map/phases/pallas_call | solution.py:299
  62.5 0.2 cosine_multiply_fusion.2
  62.7 0.2 subtract_convert_fusion.1
  62.9 19.7 %all-to-all-done = bf16[512,8,128]{2,1,0:T(8,128)(2,1)S(1)} async-done(((bf16[512,8,128]{2,1,0:T(8,128)(2,1)}), bf16[512,8,128]{2,1,0:T(8,128)(2,1)S(1)}, u32[]{:S(2)}, u32[]{:S(2)}) %all-to-all-start) | async-done | bytes 1048608 | tf_op jit(solution)/shard_map/all_to_all | solution.py:343
  82.6 10.6 %beams.1 = bf16[1024,128]{1,0:T(8,128)(2,1)S(1)} custom-call(bf16[2,4,16,4,8,128]{5,4,3,2,1,0:T(8,128)(2,1)S(1)} %bitcast.23, bf16[8,2048,256]{2,1,0:T(8,128)(2,1)} %selection.1.select_ref, bf16[2,256,512]{2,1,0:T(8,128)(2,1)S(1)} %pad_maximum_fusion.ns_ref, f32[2,32]{1,0:T(2,128)S(1)} %maximum_convert_fusion.1.ew_ref, bf16[64,64]{1,0:T(8,128)(2,1)S(1)} %bitcast.26), custom_call_target="tpu_custom_call" | custom-call | tf_op jit(solution)/shard_map/beams/pallas_call | solution.py:257
  93.1 26.8 %all_to_all.15 = bf16[512,2,128]{2,1,0:T(2,128)(2,1)S(1)} all-to-all(bf16[512,2,128]{2,1,0:T(2,128)(2,1)S(1)} %bitcast.25), channel_id=1, replica_groups=mesh['y'=8,'z_lo'=2,'z_hi'=4,'x'=4,'core'=2] {'core','z_hi','z_lo','y','x'}, dimensions={0} | all-to-all | bytes 524288 | tf_op jit(solution)/shard_map/all_to_all | solution.py:360
  119.9 1.6 %search.1 = bf16[512,128]{1,0:T(8,128)(2,1)} custom-call(bf16[1024,128]{1,0:T(8,128)(2,1)S(1)} %bitcast.24, bf16[2,1024,1024]{2,1,0:T(8,128)(2,1)S(1)} %copy-done), custom_call_target="tpu_custom_call" | custom-call | tf_op jit(solution)/shard_map/search/pallas_call | solution.py:325
  121.5 3.5 %all-to-all-start.2 = ((bf16[16,32,128]{2,1,0:T(8,128)(2,1)}), bf16[16,32,128]{2,1,0:T(8,128)(2,1)S(1)}, u32[]{:S(2)}, u32[]{:S(2)}) async-start(bf16[16,32,128]{2,1,0:T(8,128)(2,1)} %bitcast.11), calls=%async_computation.2 | async-start | bytes 262144 | tf_op jit(solution)/shard_map/all_to_all | solution.py:362
  125.1 0.1 mul.598
  125.2 0.1 copy.9
  125.3 0.1 copy_multiply_fusion
  125.4 8.4 %all-to-all-done.2 = bf16[16,32,128]{2,1,0:T(8,128)(2,1)S(1)} async-done(((bf16[16,32,128]{2,1,0:T(8,128)(2,1)}), bf16[16,32,128]{2,1,0:T(8,128)(2,1)S(1)}, u32[]{:S(2)}, u32[]{:S(2)}) %all-to-all-start.2) | async-done | bytes 131104 | tf_op jit(solution)/shard_map/all_to_all | solution.py:362
  133.8 0.2 reshape.397
  134.0 1.3 convolution_bitcast_fusion
  (31 shorter events, 0.7 us)
Async XLA Ops:
  1.5 18.7 %collective-permute-start = (bf16[64,6144]{1,0:T(8,128)(2,1)S(1)}, bf16[64,6144]{1,0:T(8,128)(2,1)S(1)}, u32[]{:S(2)}, u32[]{:S(2)}) collective-permute-start(bf16[64,6144]{1,0:T(8,128)(2,1)S(1)} %slice_convert_fusion), channel_id=1, source_target_pairs={{0,32},{32,64},{64,96},{96,128},{128,160},{160,192},{192,224},{224... | collective-permute-start | bytes 2359304 | tf_op jit(solution)/shard_map/ppermute | solution.py:340
  10.0 1.6 %copy-start.1 = (s32[64,8192]{1,0:T(8,128)S(1)}, s32[64,8192]{1,0:T(8,128)}, u32[]{:S(2)}) copy-start(s32[64,8192]{1,0:T(8,128)} %v_ref.1) | copy-start | bytes 6291460
  12.0 38.6 %copy-start.3 = (s32[2048]{0:T(1024)S(1)}, s32[2048]{0:T(1024)}, u32[]{:S(2)}) copy-start(s32[2048]{0:T(1024)} %param.6) | copy-start | bytes 24580
  20.2 36.3 %copy-start.2 = (s32[1024,512]{1,0:T(8,128)S(1)}, s32[1024,512]{1,0:T(8,128)}, u32[]{:S(2)}) copy-start(s32[1024,512]{1,0:T(8,128)} %d_ref.1) | copy-start | bytes 6291460
  23.5 59.0 %all-to-all-start = ((bf16[512,8,128]{2,1,0:T(8,128)(2,1)}), bf16[512,8,128]{2,1,0:T(8,128)(2,1)S(1)}, u32[]{:S(2)}, u32[]{:S(2)}) async-start(bf16[512,8,128]{2,1,0:T(8,128)(2,1)} %bitcast.1), calls=%async_computation | async-start | bytes 2097152 | tf_op jit(solution)/shard_map/all_to_all | solution.py:343
  82.6 37.3 %copy-start = (bf16[2,1024,1024]{2,1,0:T(8,128)(2,1)S(1)}, bf16[2,1024,1024]{2,1,0:T(8,128)(2,1)}, u32[]{:S(2)}) copy-start(bf16[2,1024,1024]{2,1,0:T(8,128)(2,1)} %phases.1.t_ref) | copy-start | bytes 12582916
  121.5 12.2 %all-to-all-start.2 = ((bf16[16,32,128]{2,1,0:T(8,128)(2,1)}), bf16[16,32,128]{2,1,0:T(8,128)(2,1)S(1)}, u32[]{:S(2)}, u32[]{:S(2)}) async-start(bf16[16,32,128]{2,1,0:T(8,128)(2,1)} %bitcast.11), calls=%async_computation.2 | async-start | bytes 262144 | tf_op jit(solution)/shard_map/all_to_all | solution.py:362

commit v6 on v5

--- a/solution.py
+++ b/solution.py
@@ -160,11 +160,11 @@
 
 
 def select_kernel(slot_ref, o_ref):
-    slots = slot_ref[pl.ds(pl.program_id(0), 1), :]
+    slots = jnp.concatenate([slot_ref[pl.ds(2 * pl.program_id(0) + pol, 1), :] for pol in range(2)], axis=1)
 
     def rows(j, _):
         at = pl.ds(pl.multiple_of(j * 256, 256), 256)
-        feed = iota((256, 256), 0) + j * 256
+        feed = iota((256, 512), 0) + j * 256
         o_ref[0, at, :] = jnp.where(feed == slots, 1.0, 0.0).astype(BF16)
         return 0
 
@@ -174,10 +174,10 @@
 def selection(slots):
     return pl.pallas_call(
         select_kernel,
-        grid=(8,),
+        grid=(4,),
         in_specs=[VMEM],
-        out_specs=pl.BlockSpec((1, 2048, 256), lambda i: (i, 0, 0)),
-        out_shape=pltpu.HBM((8, 2048, 256), BF16),
+        out_specs=pl.BlockSpec((1, 2048, 512), lambda i: (i, 0, 0)),
+        out_shape=pltpu.HBM((4, 2048, 512), BF16),
         compiler_params=LEAN,
         name="selection",
     )(slots)
@@ -203,7 +203,8 @@
         order = jnp.where(source == iota((256, 256), 1), 1.0, 0.0).astype(BF16)
         x_ref[...] = jnp.dot(order, z_ref[...], preferred_element_type=F32).astype(BF16)
 
-    grids = [jnp.dot(x_ref[...], select_ref[pol], preferred_element_type=F32).astype(BF16) for pol in range(2)]
+    both_pol = jnp.dot(x_ref[...], select_ref[0], preferred_element_type=F32).astype(BF16)
+    grids = [both_pol[:, :256], both_pol[:, 256:]]
     cyl = pl.program_id(0)
     for c in range(2):
         rows = jnp.concatenate([grid[c * 128 : (c + 1) * 128] for grid in grids], axis=0)
@@ -257,7 +258,7 @@
     return pl.pallas_call(
         beam_kernel,
         grid=(4,),
-        in_specs=[VMEM, pl.BlockSpec((2, 2048, 256), lambda i: (i, 0, 0)), VMEM, SMEM, VMEM],
+        in_specs=[VMEM, pl.BlockSpec((1, 2048, 512), lambda i: (i, 0, 0)), VMEM, SMEM, VMEM],
         out_specs=VMEM,
         out_shape=jax.ShapeDtypeStruct((1024, 128), BF16),
         scratch_shapes=[

time: 136 us -> 136 us (level)
  transfers between devices with their start and end apart: 3 -> 3, of which waited for: 3 -> 3; matrix products, arithmetic and copies ran while one was open for 5% -> 5% of each run, Pallas kernels for 9% -> 8%
where the time goes in v6:
time: 136 us; the launch traced here: 135 us
  starting transfers between devices  35.2 us (26%)
  waiting for transfers between devices  35.2 us (26%)
  blocking collectives  26.8 us (20%)
  Pallas kernels  26.1 us (19%)
  other arithmetic  8.12 us (6%)
  local copies, waits for them, and re-layouts  2.45 us (2%)
    all_to_all x1, starting transfers between devices, local(): lax.all_to_all(spectra, everyone, split_axis=0, concat_axis=0, tiled=True)  26.8 us
    all_to_all x1, blocking collectives, local(): lax.all_to_all(freq.reshape(512, 2, 128), everyone, split_axis=0, concat_...  26.8 us
    all_to_all x1, waiting for transfers between devices, local(): lax.all_to_all(spectra, everyone, split_axis=0, concat_axis=0, tiled=True)  20.9 us
    pallas_call x1, Pallas kernels, form_beams(): pl.pallas_call(beam_kernel, grid=(4,), in_specs=[VMEM, pl.BlockSpec((1, 2...  10.6 us
    all_to_all x1, waiting for transfers between devices, local(): lax.all_to_all(moved.reshape(16, 32, 128), TIME, split_axis=0, concat_axi...  8.39 us
    pallas_call x1, Pallas kernels, phase_tables(): pl.pallas_call(phase_kernel, grid=(4,), in_specs=[SMEM, pl.BlockSpec((CHA...  5.88 us
    ppermute x1, waiting for transfers between devices, local(): halo = lax.ppermute(tail, TIME, [(i, i + 1) for i in range(15)])  5.87 us
    ppermute x1, starting transfers between devices, local(): halo = lax.ppermute(tail, TIME, [(i, i + 1) for i in range(15)])  4.86 us
  transfers between devices with their start and end apart: 3, of which 3 were waited for; matrix products, arithmetic and copies ran while one was open for 5% of the time, Pallas kernels for 8%

profile of v6, /device:TPU:1, one launch (start us, length us, event | category | flops | bytes accessed | tf_op | source)
XLA Modules:
  0.0 135.3 jit_solution(7906637604585464497)
XLA Ops:
  0.0 1.5 %slice_convert_fusion = bf16[64,6144]{1,0:T(8,128)(2,1)S(1)} fusion(s32[64,8192]{1,0:T(8,128)} %v_ref.1), kind=kLoop, calls=%fused_computation.1 | loop fusion | flops 393216 | bytes 2359296 | tf_op jit(solution)/shard_map/convert.1
  1.5 4.9 %collective-permute-start = (bf16[64,6144]{1,0:T(8,128)(2,1)S(1)}, bf16[64,6144]{1,0:T(8,128)(2,1)S(1)}, u32[]{:S(2)}, u32[]{:S(2)}) collective-permute-start(bf16[64,6144]{1,0:T(8,128)(2,1)S(1)} %slice_convert_fusion), channel_id=1, source_target_pairs={{0,32},{32,64},{64,96},{96,128},{128,160},{160,192},{192,224},{224... | collective-permute-start | bytes 2359304 | tf_op jit(solution)/shard_map/ppermute | solution.py:341
  6.4 0.5 fusion.10
  7.0 0.4 multiply_reduce_fusion
  7.4 0.8 iota_multiply_fusion
  8.1 0.3 sine_multiply_fusion.1
  8.5 0.3 divide_multiply_fusion.w_ref
  8.8 1.1 sine_multiply_fusion
  10.0 1.6 %copy-done.1 = s32[64,8192]{1,0:T(8,128)S(1)} copy-done((s32[64,8192]{1,0:T(8,128)S(1)}, s32[64,8192]{1,0:T(8,128)}, u32[]{:S(2)}) %copy-start.1) | copy-done | bytes 2097176
  11.6 0.5 prefilter.1.p_ref
  12.0 0.7 iota_multiply_fusion.1
  12.8 1.5 %subtract_convert_fusion = bf16[2,32,32,1024]{3,2,1,0:T(8,128)(2,1)S(1)} fusion(f32[2,32,1024]{2,1,0:T(8,128)S(1)} %get-tuple-element.18, f32[32,1024]{1,0:T(8,128)S(1)} %get-tuple-element.17, f32[2,32,1024]{2,1,0:T(8,128)S(1)} %get-tuple-element.16, f32[32,1024]{1,0:T(8,128)S(1)} %get-tuple-element.15), kind=kLoop, calls=%fused_computation | loop fusion | flops 8388608 | bytes 4980736 | tf_op jit(solution)/shard_map/convert_element_type | solution.py:55
  14.3 5.9 %collective-permute-done.h_ref = bf16[64,6144]{1,0:T(8,128)(2,1)S(1)} collective-permute-done((bf16[64,6144]{1,0:T(8,128)(2,1)S(1)}, bf16[64,6144]{1,0:T(8,128)(2,1)S(1)}, u32[]{:S(2)}, u32[]{:S(2)}) %collective-permute-start) | collective-permute-done | bytes 786464 | tf_op jit(solution)/shard_map/ppermute | solution.py:341
  20.2 3.4 %channelize.1 = bf16[256,2,8,128]{3,2,1,0:T(8,128)(2,1)} custom-call(f32[4,64,2048]{2,1,0:T(8,128)S(1)} %prefilter.1.p_ref, bf16[64,6144]{1,0:T(8,128)(2,1)S(1)} %collective-permute-done.h_ref, f32[4,2048]{1,0:T(4,128)S(1)} %divide_multiply_fusion.w_ref, bf16[4,512,1024]{2,1,0:T(8,128)(2,1)S(1)} %bitcast.22), custom_call_target="tpu_custom_call" | custom-call | tf_op jit(solution)/shard_map/channelize/pallas_call | solution.py:150
  23.5 26.8 %all-to-all-start = ((bf16[512,8,128]{2,1,0:T(8,128)(2,1)}), bf16[512,8,128]{2,1,0:T(8,128)(2,1)S(1)}, u32[]{:S(2)}, u32[]{:S(2)}) async-start(bf16[512,8,128]{2,1,0:T(8,128)(2,1)} %bitcast.1), calls=%async_computation | async-start | bytes 2097152 | tf_op jit(solution)/shard_map/all_to_all | solution.py:344
  50.4 0.1 mul.585
  50.6 0.1 reshape.393
  50.8 4.2 %selection.1.select_ref = bf16[4,2048,512]{2,1,0:T(8,128)(2,1)} custom-call(s32[8,256]{1,0:T(8,128)S(1)} %bitcast.28), custom_call_target="tpu_custom_call" | custom-call | tf_op jit(solution)/shard_map/selection/pallas_call | solution.py:175
  55.2 5.9 %phases.1.t_ref = bf16[2,1024,1024]{2,1,0:T(8,128)(2,1)} custom-call(s32[2]{0:T(128)S(1)} %pad_add_fusion.1.num_ref, s32[1024,512]{1,0:T(8,128)S(1)} %copy-done.2, f32[8,128]{1,0:T(8,128)S(1)} %maximum_maximum_fusion.lut_ref), custom_call_target="tpu_custom_call" | custom-call | tf_op jit(solution)/shard_map/phases/pallas_call | solution.py:300
  61.3 0.2 cosine_multiply_fusion.2
  61.4 0.2 subtract_convert_fusion.1
  61.7 20.9 %all-to-all-done = bf16[512,8,128]{2,1,0:T(8,128)(2,1)S(1)} async-done(((bf16[512,8,128]{2,1,0:T(8,128)(2,1)}), bf16[512,8,128]{2,1,0:T(8,128)(2,1)S(1)}, u32[]{:S(2)}, u32[]{:S(2)}) %all-to-all-start) | async-done | bytes 1048608 | tf_op jit(solution)/shard_map/all_to_all | solution.py:344
  82.6 10.6 %beams.1 = bf16[1024,128]{1,0:T(8,128)(2,1)S(1)} custom-call(bf16[2,4,16,4,8,128]{5,4,3,2,1,0:T(8,128)(2,1)S(1)} %bitcast.23, bf16[4,2048,512]{2,1,0:T(8,128)(2,1)} %selection.1.select_ref, bf16[2,256,512]{2,1,0:T(8,128)(2,1)S(1)} %pad_maximum_fusion.ns_ref, f32[2,32]{1,0:T(2,128)S(1)} %maximum_convert_fusion.1.ew_ref, bf16[64,64]{1,0:T(8,128)(2,1)S(1)} %bitcast.26), custom_call_target="tpu_custom_call" | custom-call | tf_op jit(solution)/shard_map/beams/pallas_call | solution.py:258
  93.1 26.8 %all_to_all.15 = bf16[512,2,128]{2,1,0:T(2,128)(2,1)S(1)} all-to-all(bf16[512,2,128]{2,1,0:T(2,128)(2,1)S(1)} %bitcast.25), channel_id=1, replica_groups=mesh['y'=8,'z_lo'=2,'z_hi'=4,'x'=4,'core'=2] {'core','z_hi','z_lo','y','x'}, dimensions={0} | all-to-all | bytes 524288 | tf_op jit(solution)/shard_map/all_to_all | solution.py:361
  119.9 1.6 %search.1 = bf16[512,128]{1,0:T(8,128)(2,1)} custom-call(bf16[1024,128]{1,0:T(8,128)(2,1)S(1)} %bitcast.24, bf16[2,1024,1024]{2,1,0:T(8,128)(2,1)S(1)} %copy-done), custom_call_target="tpu_custom_call" | custom-call | tf_op jit(solution)/shard_map/search/pallas_call | solution.py:326
  121.5 3.5 %all-to-all-start.2 = ((bf16[16,32,128]{2,1,0:T(8,128)(2,1)}), bf16[16,32,128]{2,1,0:T(8,128)(2,1)S(1)}, u32[]{:S(2)}, u32[]{:S(2)}) async-start(bf16[16,32,128]{2,1,0:T(8,128)(2,1)} %bitcast.11), calls=%async_computation.2 | async-start | bytes 262144 | tf_op jit(solution)/shard_map/all_to_all | solution.py:363
  125.1 0.1 mul.598
  125.2 0.1 copy.9
  125.3 0.1 copy_multiply_fusion
  125.4 8.4 %all-to-all-done.2 = bf16[16,32,128]{2,1,0:T(8,128)(2,1)S(1)} async-done(((bf16[16,32,128]{2,1,0:T(8,128)(2,1)}), bf16[16,32,128]{2,1,0:T(8,128)(2,1)S(1)}, u32[]{:S(2)}, u32[]{:S(2)}) %all-to-all-start.2) | async-done | bytes 131104 | tf_op jit(solution)/shard_map/all_to_all | solution.py:363
  133.8 0.2 reshape.397
  134.0 1.3 convolution_bitcast_fusion
  (31 shorter events, 0.7 us)
Async XLA Ops:
  1.5 18.7 %collective-permute-start = (bf16[64,6144]{1,0:T(8,128)(2,1)S(1)}, bf16[64,6144]{1,0:T(8,128)(2,1)S(1)}, u32[]{:S(2)}, u32[]{:S(2)}) collective-permute-start(bf16[64,6144]{1,0:T(8,128)(2,1)S(1)} %slice_convert_fusion), channel_id=1, source_target_pairs={{0,32},{32,64},{64,96},{96,128},{128,160},{160,192},{192,224},{224... | collective-permute-start | bytes 2359304 | tf_op jit(solution)/shard_map/ppermute | solution.py:341
  10.0 1.6 %copy-start.1 = (s32[64,8192]{1,0:T(8,128)S(1)}, s32[64,8192]{1,0:T(8,128)}, u32[]{:S(2)}) copy-start(s32[64,8192]{1,0:T(8,128)} %v_ref.1) | copy-start | bytes 6291460
  12.0 38.6 %copy-start.3 = (s32[2048]{0:T(1024)S(1)}, s32[2048]{0:T(1024)}, u32[]{:S(2)}) copy-start(s32[2048]{0:T(1024)} %param.6) | copy-start | bytes 24580
  20.2 35.1 %copy-start.2 = (s32[1024,512]{1,0:T(8,128)S(1)}, s32[1024,512]{1,0:T(8,128)}, u32[]{:S(2)}) copy-start(s32[1024,512]{1,0:T(8,128)} %d_ref.1) | copy-start | bytes 6291460
  23.5 59.0 %all-to-all-start = ((bf16[512,8,128]{2,1,0:T(8,128)(2,1)}), bf16[512,8,128]{2,1,0:T(8,128)(2,1)S(1)}, u32[]{:S(2)}, u32[]{:S(2)}) async-start(bf16[512,8,128]{2,1,0:T(8,128)(2,1)} %bitcast.1), calls=%async_computation | async-start | bytes 2097152 | tf_op jit(solution)/shard_map/all_to_all | solution.py:344
  82.6 37.3 %copy-start = (bf16[2,1024,1024]{2,1,0:T(8,128)(2,1)S(1)}, bf16[2,1024,1024]{2,1,0:T(8,128)(2,1)}, u32[]{:S(2)}) copy-start(bf16[2,1024,1024]{2,1,0:T(8,128)(2,1)} %phases.1.t_ref) | copy-start | bytes 12582916
  121.5 12.2 %all-to-all-start.2 = ((bf16[16,32,128]{2,1,0:T(8,128)(2,1)}), bf16[16,32,128]{2,1,0:T(8,128)(2,1)S(1)}, u32[]{:S(2)}, u32[]{:S(2)}) async-start(bf16[16,32,128]{2,1,0:T(8,128)(2,1)} %bitcast.11), calls=%async_computation.2 | async-start | bytes 262144 | tf_op jit(solution)/shard_map/all_to_all | solution.py:363
